TPU v7x, 512 devices: a whole 4x8x8 slice. The times are simulated.
512 devices in a mesh: energy: 128 (over x_lo, z, y), space: 4 (over x_hi, core).
Axes of the slice: x: 4 (x_hi: 2, x_lo: 2; x = x_hi * 2 + x_lo), y: 8, z: 8, core: 2. Of those that a mesh axis runs over, the one named last changes fastest.
Arguments:
- greens: bfloat16 [128, 8, 3, 2, 128, 128], P('energy', 'space'), may hold values from -6 to 6
- coulomb: bfloat16 [8, 5, 128, 128], replicated, may hold values from -0.25 to 0.25
- band_mask: int32 [8, 5], replicated, may hold values 0 or 1
- window_lo: int32 [8], replicated, may hold values from 0 to 64
Outputs:
- greens_next: bfloat16 [128, 8, 3, 2, 128, 128], P('energy', 'space')
All inputs are finite; a program needn't handle non-finite values.
Results may differ from a plain program's by a relative error of at most 0.0095.
Values may be sent and summed in bfloat16 or wider, within the bound.
A program may use at most 128 MiB of HBM per device.

v0:
```python
import math

import jax
import jax.numpy as jnp
from jax import lax
from jax.sharding import PartitionSpec as P


def in_blocks(x, dim, size):
    shape = x.shape
    blocks = x.reshape(*shape[:dim], size, shape[dim] // size, *shape[dim + 1 :])
    return jnp.moveaxis(blocks, dim, 0)


def piece_ends(length, count):
    step = length // count
    if step >= 8:
        step -= step % 8
    return [step * k for k in range(1, count)]


def in_order(blocks, dim):
    shape = list(blocks.shape[1:])
    shape[dim] *= blocks.shape[0]
    return jnp.moveaxis(blocks, 0, dim).reshape(shape)


def exchange_in_pieces(x, axis, pieces, split_dim, concat_dim):
    blocks = in_blocks(x, split_dim, lax.axis_size(axis))
    split_at = max(range(1, max(2, blocks.ndim - 1)), key=lambda d: blocks.shape[d])
    finished = []
    for section in jnp.split(blocks, piece_ends(blocks.shape[split_at], pieces), axis=split_at):
        if section.size:
            finished.append(lax.all_to_all(section, axis, split_axis=0, concat_axis=0, tiled=True))
    return in_order(jnp.concatenate(finished, axis=split_at), concat_dim)


def padded_2(x, sides, width):
    for axis, dim in sides:
        size, length = (lax.axis_size(axis), x.shape[dim])
        up = [(i, (i + 1) % size) for i in range(size - 1)]
        down = [(j, i) for i, j in up]
        last = lax.slice_in_dim(x, length - width, length, axis=dim)
        initial = lax.slice_in_dim(x, 0, width, axis=dim)
        before = lax.ppermute(last, axis, up)
        after = lax.ppermute(initial, axis, down)
        x = jnp.concatenate([before, x, after], axis=dim)
    return x


def to_elements(blocks):
    return exchange_in_pieces(blocks, "energy", 2, 4, 0)


def to_energies(blocks):
    return lax.all_to_all(blocks, "energy", split_axis=0, concat_axis=4, tiled=True)


def with_rims(stacked):
    return padded_2(stacked, (("space", 2),), 2)


def band_tile(store, shift, offset, row_count):
    if offset >= 0:
        return (store[:, 2 + shift : 2 + shift + row_count, offset], False)
    start = 2 + shift + offset
    return (store[:, start : start + row_count, -offset], True)


def oriented(tile, flipped):
    return jnp.swapaxes(tile, -1, -2) if flipped else tile


def complex_joined(lefts, rights):
    left = jnp.concatenate(lefts, axis=-1)
    right = jnp.concatenate(rights, axis=-2)
    left_re = left[:, :, 0]
    left_im = left[:, :, 1]
    rows_re = jnp.concatenate([left_re, -left_im], axis=-1)
    rows_im = jnp.concatenate([left_im, left_re], axis=-1)
    wide_left = jnp.stack([rows_re, rows_im], axis=2)
    tall_right = jnp.concatenate([right[:, :, 0], right[:, :, 1]], axis=-2)
    return jnp.einsum(
        "ercik,erkj->ercij", wide_left, tall_right, preferred_element_type=jnp.float32
    )


def screened_band(polar_window, coulomb_window, row_count):
    partial_rows = {}
    for extent in range(-2, 5):
        lefts = []
        rights = []
        for middle in range(-2, 3):
            second = extent - middle
            if -2 <= second <= 2:
                lefts.append(coulomb_window[2 : 2 + row_count, middle + 2])
                piece, flipped = band_tile(polar_window, middle, second, row_count)
                rights.append(oriented(piece, flipped))
        left = jnp.concatenate(lefts, axis=-1)
        right = jnp.concatenate(rights, axis=-2)
        partial_rows[extent] = jnp.einsum(
            "rik,erckj->ercij", left, right, preferred_element_type=jnp.float32
        ).astype(jnp.bfloat16)
    results = []
    for column in range(3):
        lefts = []
        rights = []
        for extent in range(column - 2, column + 3):
            coulomb_tile = coulomb_window[2 + column : 2 + column + row_count, extent - column + 2]
            lefts.append(partial_rows[extent])
            rights.append(jnp.swapaxes(coulomb_tile, -1, -2))
        left = jnp.concatenate(lefts, axis=-1)
        right = jnp.concatenate(rights, axis=-2)
        results.append(
            jnp.einsum("ercik,rkj->ercij", left, right, preferred_element_type=jnp.float32)
        )
    return jnp.stack(results, axis=2)


def dyson_band(green_window, sigma_window, row_count, coupling):
    left_products = {}
    for extent in range(-2, 5):
        lefts = []
        rights = []
        for middle in range(-2, 3):
            second = extent - middle
            if -2 <= second <= 2:
                green_tile, green_flip = band_tile(green_window, 0, middle, row_count)
                sigma_tile, sigma_flip = band_tile(sigma_window, middle, second, row_count)
                lefts.append(oriented(green_tile, green_flip))
                rights.append(oriented(sigma_tile, sigma_flip))
        left_products[extent] = complex_joined(lefts, rights).astype(jnp.bfloat16)
    results = []
    for column in range(3):
        lefts = []
        rights = []
        for extent in range(column - 2, column + 3):
            green_tile, green_flip = band_tile(green_window, extent, column - extent, row_count)
            lefts.append(left_products[extent])
            rights.append(oriented(green_tile, green_flip))
        summed = complex_joined(lefts, rights)
        base_tile = green_window[:, 2 : 2 + row_count, column].astype(jnp.float32)
        results.append(base_tile + coupling * summed)
    return jnp.stack(results, axis=2).astype(jnp.bfloat16)


def split_pair(values):
    upper = values.astype(jnp.bfloat16)
    widened = lax.optimization_barrier(upper).astype(jnp.float32)
    lower = (values - widened).astype(jnp.bfloat16)
    return (upper, lower)


def fourier_table(points):
    length = 2 * points
    frequency = lax.broadcasted_iota(jnp.int32, (length, points), 0)
    energy_steps = lax.broadcasted_iota(jnp.int32, (length, points), 1)
    phases = (frequency * energy_steps % length).astype(jnp.float32) * (2.0 * math.pi / length)
    return split_pair(jnp.concatenate([jnp.cos(phases), jnp.sin(phases)], axis=0))


def transform(lookup, blocks):
    upper, lower = lookup
    points = blocks.shape[0]
    length = 2 * points
    real_part = blocks[:, :, :, 0].reshape(points, -1)
    imag_part = blocks[:, :, :, 1].reshape(points, -1)
    columns = real_part.shape[1]
    values = jnp.concatenate([real_part, imag_part], axis=1)
    spectrum = jnp.dot(upper, values, preferred_element_type=jnp.float32) + jnp.dot(
        lower, values, preferred_element_type=jnp.float32
    )
    cos_re = spectrum[:length, :columns]
    cos_im = spectrum[:length, columns:]
    sin_re = spectrum[length:, :columns]
    sin_im = spectrum[length:, columns:]
    return (cos_re, sin_im, cos_im, sin_re)


def inverse_pair(lookup, spectrum_real, spectrum_imag, factor_scale):
    upper, lower = lookup
    columns = spectrum_real.shape[1]
    stacked = jnp.concatenate(
        [
            jnp.concatenate([spectrum_real, spectrum_imag], axis=1),
            jnp.concatenate([-spectrum_imag, spectrum_real], axis=1),
        ],
        axis=0,
    )
    value_upper, value_lower = split_pair(stacked)
    total = jnp.einsum("ke,kn->en", upper, value_upper, preferred_element_type=jnp.float32)
    total = total + jnp.einsum("ke,kn->en", upper, value_lower, preferred_element_type=jnp.float32)
    total = total + jnp.einsum("ke,kn->en", lower, value_upper, preferred_element_type=jnp.float32)
    total = total * factor_scale
    return (total[:, :columns], total[:, columns:])


def assemble(real_part, imag_part, out_shape):
    inner_shape = (out_shape[0], out_shape[1], out_shape[2], out_shape[4])
    return jnp.stack([real_part.reshape(inner_shape), imag_part.reshape(inner_shape)], axis=3)


def on_device(greens, coulomb, band_mask, window_lo):
    energy_local = greens.shape[0]
    row_count = greens.shape[1]
    width = greens.shape[-1]
    rows_all = band_mask.shape[0]
    first_row = lax.axis_index("space") * row_count
    tile_rows = first_row + lax.broadcasted_iota(jnp.int32, (row_count, 3), 0)
    tile_offsets = lax.broadcasted_iota(jnp.int32, (row_count, 3), 1)
    kept_tiles = (tile_rows + tile_offsets < rows_all).astype(jnp.bfloat16)
    greens = greens * kept_tiles[None, :, :, None, None, None]
    coulomb_rows = lax.broadcasted_iota(jnp.int32, (rows_all, 5), 0)
    coulomb_offsets = lax.broadcasted_iota(jnp.int32, (rows_all, 5), 1) - 2
    inside = (
        (coulomb_rows + coulomb_offsets >= 0)
        & (coulomb_rows + coulomb_offsets < rows_all)
        & (band_mask > 0)
    )
    masked = coulomb * inside.astype(jnp.bfloat16)[:, :, None, None]
    padded = jnp.pad(masked, ((2, 2), (0, 0), (0, 0), (0, 0)))
    coulomb_window = lax.dynamic_slice_in_dim(padded, first_row, row_count + 4, 0)
    flat_shape = (energy_local, row_count, 3, 2, width * width)
    full_shape = (energy_local, row_count, 3, 2, width, width)
    element_slabs = to_elements(greens.reshape(flat_shape))
    energies = element_slabs.shape[0]
    lookup = fourier_table(energies)
    factor_scale = 1.0 / (2 * energies * math.sqrt(energies))
    cos_re, sin_im, cos_im, sin_re = transform(lookup, element_slabs)
    green_re = cos_re + sin_im
    green_im = cos_im - sin_re
    mirror_re = cos_re - sin_im
    mirror_im = cos_im + sin_re
    polar_re = green_re * mirror_re - green_im * mirror_im
    polar_im = green_re * mirror_im + green_im * mirror_re
    polar_real, polar_imag = inverse_pair(lookup, polar_re, polar_im, factor_scale)
    polar_slabs = assemble(polar_real, polar_imag, element_slabs.shape).astype(jnp.bfloat16)
    polarization = to_energies(polar_slabs).reshape(full_shape)
    joined = with_rims(jnp.stack([polarization, greens]))
    polar_window = joined[0]
    green_window = joined[1]
    screened = screened_band(polar_window, coulomb_window, row_count).astype(jnp.bfloat16)
    screen_slabs = to_elements(screened.reshape(flat_shape))
    screen_cos_re, screen_sin_im, screen_cos_im, screen_sin_re = transform(lookup, screen_slabs)
    screen_re = screen_cos_re + screen_sin_im
    screen_im = screen_cos_im - screen_sin_re
    sigma_re = green_re * screen_re - green_im * screen_im
    sigma_im = green_re * screen_im + green_im * screen_re
    sigma_real, sigma_imag = inverse_pair(lookup, sigma_re, sigma_im, factor_scale)
    sigma_slabs = assemble(sigma_real, sigma_imag, element_slabs.shape)
    energy_ids = lax.broadcasted_iota(jnp.int32, (energies, row_count), 0)
    window_start = lax.dynamic_slice_in_dim(window_lo, first_row, row_count, 0)[None, :]
    active = ((energy_ids >= window_start) & (energy_ids < window_start + energies // 2)).astype(
        jnp.float32
    )
    sigma_slabs = (sigma_slabs * active[:, :, None, None, None]).astype(jnp.bfloat16)
    self_energy = to_energies(sigma_slabs).reshape(full_shape)
    sigma_window = with_rims(self_energy[None])[0]
    return dyson_band(green_window, sigma_window, row_count, 1.0 / (5 * width))


def solution(mesh):
    return jax.shard_map(
        on_device,
        mesh=mesh,
        in_specs=(P("energy", "space", None, None, None, None), P(), P(), P()),
        out_specs=P("energy", "space", None, None, None, None),
        check_vma=False,
    )
```

profile of v0, /device:TPU:1, one launch (start us, length us, event | category | flops | bytes accessed | tf_op | source)
XLA Modules:
  0.0 263.5 jit_solution(7921070082554327820)
XLA Ops:
  0.0 1.2 copy.159
  2.9 19.3 %all-to-all-start = ((bf16[128,1,2,1,2,128]{5,4,2,3,1,0:T(2,128)(2,1)}), bf16[128,1,2,1,2,128]{5,4,2,3,1,0:T(2,128)(2,1)S(1)}, u32[]{:S(2)}, u32[]{:S(2)}) async-start(bf16[128,1,2,1,2,128]{5,4,2,3,1,0:T(2,128)(2,1)} %copy.160), calls=%async_computation | async-start | bytes 262144 | tf_op jit(solution)/shard_map/all_to_all | solution.py:34
  22.9 1.5 copy_multiply_fusion
  26.3 8.0 %all-to-all-done = bf16[128,1,2,1,2,128]{5,4,2,3,1,0:T(2,128)(2,1)S(1)} async-done(((bf16[128,1,2,1,2,128]{5,4,2,3,1,0:T(2,128)(2,1)}), bf16[128,1,2,1,2,128]{5,4,2,3,1,0:T(2,128)(2,1)S(1)}, u32[]{:S(2)}, u32[]{:S(2)}) %all-to-all-start) | async-done | bytes 131104 | tf_op jit(solution)/shard_map/all_to_all | solution.py:34
  34.4 6.2 %all-to-all-start.1 = ((bf16[128,1,2,2,2,128]{5,4,2,3,1,0:T(2,128)(2,1)}), bf16[128,1,2,2,2,128]{5,4,2,3,1,0:T(2,128)(2,1)S(1)}, u32[]{:S(2)}, u32[]{:S(2)}) async-start(bf16[128,1,2,2,2,128]{5,4,2,3,1,0:T(2,128)(2,1)} %copy.161), calls=%async_computation.1 | async-start | bytes 524288 | tf_op jit(solution)/shard_map/all_to_all | solution.py:34
  43.5 10.5 %all-to-all-done.1 = bf16[128,1,2,2,2,128]{5,4,2,3,1,0:T(2,128)(2,1)S(1)} async-done(((bf16[128,1,2,2,2,128]{5,4,2,3,1,0:T(2,128)(2,1)}), bf16[128,1,2,2,2,128]{5,4,2,3,1,0:T(2,128)(2,1)S(1)}, u32[]{:S(2)}, u32[]{:S(2)}) %all-to-all-start.1) | async-done | bytes 262176 | tf_op jit(solution)/shard_map/all_to_all | solution.py:34
  58.5 1.1 copy.166
  59.6 7.2 %all-to-all-start.2 = ((bf16[128,2,3,2,128]{4,3,1,2,0:T(2,128)(2,1)}), bf16[128,2,3,2,128]{4,3,1,2,0:T(2,128)(2,1)S(1)}, u32[]{:S(2)}, u32[]{:S(2)}) async-start(bf16[128,2,3,2,128]{4,3,1,2,0:T(2,128)(2,1)} %copy.166), calls=%async_computation.2 | async-start | bytes 786432 | tf_op jit(solution)/shard_map/all_to_all | solution.py:56
  67.7 14.2 %all-to-all-done.2 = bf16[128,2,3,2,128]{4,3,1,2,0:T(2,128)(2,1)S(1)} async-done(((bf16[128,2,3,2,128]{4,3,1,2,0:T(2,128)(2,1)}), bf16[128,2,3,2,128]{4,3,1,2,0:T(2,128)(2,1)S(1)}, u32[]{:S(2)}, u32[]{:S(2)}) %all-to-all-start.2) | async-done | bytes 393248 | tf_op jit(solution)/shard_map/all_to_all | solution.py:56
  82.7 8.6 %collective-permute-start = (bf16[2,1,2,3,2,128,128]{5,6,4,2,3,1,0:T(8,128)(2,1)S(1)}, bf16[2,1,2,3,2,128,128]{5,6,4,2,3,1,0:T(8,128)(2,1)S(1)}, u32[]{:S(2)}, u32[]{:S(2)}) collective-permute-start(bf16[2,1,2,3,2,128,128]{5,6,4,2,3,1,0:T(8,128)(2,1)S(1)} %pad_maximum_fusion.1), channel_id=1, source_target_pairs={{0,1},{1,2},{2,3},{4,5},{5,6},{6,7},{8,9},{9,10},{10,11},{12,13},{... | collective-permute-start | bytes 2359304 | tf_op jit(solution)/shard_map/ppermute | solution.py:45
  91.3 2.1 collective-permute-start.1
  96.0 4.2 %collective-permute-done = bf16[2,1,2,3,2,128,128]{5,6,4,2,3,1,0:T(8,128)(2,1)S(1)} collective-permute-done((bf16[2,1,2,3,2,128,128]{5,6,4,2,3,1,0:T(8,128)(2,1)S(1)}, bf16[2,1,2,3,2,128,128]{5,6,4,2,3,1,0:T(8,128)(2,1)S(1)}, u32[]{:S(2)}, u32[]{:S(2)}) %collective-permute-start) | collective-permute-done | bytes 786464 | tf_op jit(solution)/shard_map/ppermute | solution.py:45
  100.2 5.9 %collective-permute-done.1 = bf16[2,1,2,3,2,128,128]{5,6,4,2,3,1,0:T(8,128)(2,1)S(1)} collective-permute-done((bf16[2,1,2,3,2,128,128]{5,6,4,2,3,1,0:T(8,128)(2,1)S(1)}, bf16[2,1,2,3,2,128,128]{5,6,4,2,3,1,0:T(8,128)(2,1)S(1)}, u32[]{:S(2)}, u32[]{:S(2)}) %collective-permute-start.1) | collective-permute-done | bytes 786464 | tf_op jit(solution)/shard_map/ppermute | solution.py:46
  106.5 1.1 slice_bitcast_fusion.64
  107.7 1.0 copy.285
  108.7 1.7 copy.198
  111.1 1.2 pad_maximum_fusion.8
  122.7 1.4 slice_bitcast_fusion.52
  124.2 1.7 copy.172
  125.8 1.6 constant_dynamic-update-slice_fusion.9
  127.4 1.7 copy.287
  129.1 1.7 copy.177
  130.7 1.7 copy.289
  132.4 1.7 copy.178
  134.0 1.6 constant_dynamic-update-slice_fusion.8
  135.6 1.6 constant_dynamic-update-slice_fusion.7
  137.2 1.6 constant_dynamic-update-slice_fusion.6
  139.4 1.7 copy.173
  141.1 1.7 copy.288
  143.5 1.4 fusion.44
  150.6 6.2 %all-to-all-start.3 = ((bf16[128,1,2,1,2,128]{5,4,2,3,1,0:T(2,128)(2,1)}), bf16[128,1,2,1,2,128]{5,4,2,3,1,0:T(2,128)(2,1)S(1)}, u32[]{:S(2)}, u32[]{:S(2)}) async-start(bf16[128,1,2,1,2,128]{5,4,2,3,1,0:T(2,128)(2,1)} %copy.185), calls=%async_computation.3 | async-start | bytes 262144 | tf_op jit(solution)/shard_map/all_to_all | solution.py:34
  161.4 1.6 constant_dynamic-update-slice_fusion.73
  166.5 1.0 maximum_bitcast_fusion.49
  167.6 1.1 maximum_bitcast_fusion.33
  168.7 1.1 maximum_bitcast_fusion.29
  172.6 14.5 %all-to-all-start.4 = ((bf16[128,1,2,2,2,128]{5,4,2,3,1,0:T(2,128)(2,1)}), bf16[128,1,2,2,2,128]{5,4,2,3,1,0:T(2,128)(2,1)S(1)}, u32[]{:S(2)}, u32[]{:S(2)}) async-start(bf16[128,1,2,2,2,128]{5,4,2,3,1,0:T(2,128)(2,1)} %copy.186), calls=%async_computation.4 | async-start | bytes 524288 | tf_op jit(solution)/shard_map/all_to_all | solution.py:34
  187.4 12.9 %all-to-all-done.4 = bf16[128,1,2,2,2,128]{5,4,2,3,1,0:T(2,128)(2,1)S(1)} async-done(((bf16[128,1,2,2,2,128]{5,4,2,3,1,0:T(2,128)(2,1)}), bf16[128,1,2,2,2,128]{5,4,2,3,1,0:T(2,128)(2,1)S(1)}, u32[]{:S(2)}, u32[]{:S(2)}) %all-to-all-start.4) | async-done | bytes 262176 | tf_op jit(solution)/shard_map/all_to_all | solution.py:34
  204.9 1.1 copy.191
  206.0 6.2 %all-to-all-start.5 = ((bf16[128,2,3,2,128]{4,1,3,2,0:T(2,128)(2,1)}), bf16[128,2,3,2,128]{4,1,3,2,0:T(2,128)(2,1)S(1)}, u32[]{:S(2)}, u32[]{:S(2)}) async-start(bf16[128,2,3,2,128]{4,1,3,2,0:T(2,128)(2,1)} %copy.191), calls=%async_computation.5 | async-start | bytes 786432 | tf_op jit(solution)/shard_map/all_to_all | solution.py:56
  213.0 1.7 copy.291
  215.5 1.9 slice_bitcast_fusion.11
  219.3 7.5 %all-to-all-done.5 = bf16[128,2,3,2,128]{4,1,3,2,0:T(2,128)(2,1)S(1)} async-done(((bf16[128,2,3,2,128]{4,1,3,2,0:T(2,128)(2,1)}), bf16[128,2,3,2,128]{4,1,3,2,0:T(2,128)(2,1)S(1)}, u32[]{:S(2)}, u32[]{:S(2)}) %all-to-all-start.5) | async-done | bytes 393248 | tf_op jit(solution)/shard_map/all_to_all | solution.py:56
  227.4 4.6 %collective-permute-start.2 = (bf16[1,1,2,3,2,128,128]{5,6,2,4,3,1,0:T(8,128)(2,1)S(1)}, bf16[1,1,2,3,2,128,128]{5,6,2,4,3,1,0:T(8,128)(2,1)S(1)}, u32[]{:S(2)}, u32[]{:S(2)}) collective-permute-start(bf16[1,1,2,3,2,128,128]{5,6,2,4,3,1,0:T(8,128)(2,1)S(1)} %bitcast.731), channel_id=1, source_target_pairs={{0,1},{1,2},{2,3},{4,5},{5,6},{6,7},{8,9},{9,10},{10,11},{12,13},{... | collective-permute-start | bytes 1179656 | tf_op jit(solution)/shard_map/ppermute | solution.py:45
  232.0 2.2 collective-permute-start.3
  236.7 5.9 %collective-permute-done.3 = bf16[1,1,2,3,2,128,128]{5,6,2,4,3,1,0:T(8,128)(2,1)S(1)} collective-permute-done((bf16[1,1,2,3,2,128,128]{5,6,2,4,3,1,0:T(8,128)(2,1)S(1)}, bf16[1,1,2,3,2,128,128]{5,6,2,4,3,1,0:T(8,128)(2,1)S(1)}, u32[]{:S(2)}, u32[]{:S(2)}) %collective-permute-start.3) | collective-permute-done | bytes 393248 | tf_op jit(solution)/shard_map/ppermute | solution.py:46
  242.8 1.3 slice_bitcast_fusion.44
  246.3 1.0 copy.293
  248.3 1.0 constant_dynamic-update-slice_fusion.45
  (376 shorter events, 73.3 us)
Async XLA Ops:
  0.0 22.7 %copy-start.99 = (s32[8,5]{1,0:T(8,128)S(1)}, s32[8,5]{1,0:T(8,128)}, u32[]{:S(2)}) copy-start(s32[8,5]{1,0:T(8,128)} %param.6) | copy-start | bytes 484
  2.9 31.5 %all-to-all-start = ((bf16[128,1,2,1,2,128]{5,4,2,3,1,0:T(2,128)(2,1)}), bf16[128,1,2,1,2,128]{5,4,2,3,1,0:T(2,128)(2,1)S(1)}, u32[]{:S(2)}, u32[]{:S(2)}) async-start(bf16[128,1,2,1,2,128]{5,4,2,3,1,0:T(2,128)(2,1)} %copy.160), calls=%async_computation | async-start | bytes 262144 | tf_op jit(solution)/shard_map/all_to_all | solution.py:34
  26.3 15.6 %copy-start.52 = (bf16[2,640,128]{1,2,0:T(8,128)(2,1)}, bf16[2,640,128]{1,2,0:T(8,128)(2,1)S(1)}, u32[]{:S(2)}) copy-start(bf16[2,640,128]{1,2,0:T(8,128)(2,1)S(1)} %get-tuple-element.31) | copy-start | bytes 983044
  26.3 15.6 %copy-start.56 = (bf16[2,640,128]{1,2,0:T(8,128)(2,1)}, bf16[2,640,128]{1,2,0:T(8,128)(2,1)S(1)}, u32[]{:S(2)}) copy-start(bf16[2,640,128]{1,2,0:T(8,128)(2,1)S(1)} %get-tuple-element.28) | copy-start | bytes 983044
  34.4 19.7 %all-to-all-start.1 = ((bf16[128,1,2,2,2,128]{5,4,2,3,1,0:T(2,128)(2,1)}), bf16[128,1,2,2,2,128]{5,4,2,3,1,0:T(2,128)(2,1)S(1)}, u32[]{:S(2)}, u32[]{:S(2)}) async-start(bf16[128,1,2,2,2,128]{5,4,2,3,1,0:T(2,128)(2,1)} %copy.161), calls=%async_computation.1 | async-start | bytes 524288 | tf_op jit(solution)/shard_map/all_to_all | solution.py:34
  43.3 14.3 %copy-start.5 = (bf16[512,128]{1,0:T(8,128)(2,1)}, bf16[512,128]{1,0:T(8,128)(2,1)S(1)}, u32[]{:S(2)}) copy-start(bf16[512,128]{1,0:T(8,128)(2,1)S(1)} %subtract_convert_fusion.4) | copy-start | bytes 393220
  58.1 8.7 %copy-start.100 = (s32[8]{0:T(128)S(1)}, s32[8]{0:T(128)}, u32[]{:S(2)}) copy-start(s32[8]{0:T(128)} %param.7) | copy-start | bytes 100
  58.1 8.8 %copy-start.75 = (bf16[2,1,128,128]{3,2,0,1:T(8,128)(2,1)S(1)}, bf16[2,1,128,128]{3,2,0,1:T(8,128)(2,1)}, u32[]{:S(2)}) copy-start(bf16[2,1,128,128]{3,2,0,1:T(8,128)(2,1)} %get-tuple-element.20) | copy-start | bytes 196612
  58.1 8.8 %copy-start.77 = (bf16[2,1,128,128]{3,2,0,1:T(8,128)(2,1)S(1)}, bf16[2,1,128,128]{3,2,0,1:T(8,128)(2,1)}, u32[]{:S(2)}) copy-start(bf16[2,1,128,128]{3,2,0,1:T(8,128)(2,1)} %get-tuple-element.18) | copy-start | bytes 196612
  58.4 24.1 %copy-start.2 = (bf16[1,1,2,3,2,128,128]{5,6,4,2,3,1,0:T(8,128)(2,1)S(1)}, bf16[1,1,2,3,2,128,128]{5,6,4,2,3,1,0:T(8,128)(2,1)}, u32[]{:S(2)}) copy-start(bf16[1,1,2,3,2,128,128]{5,6,4,2,3,1,0:T(8,128)(2,1)} %get-tuple-element.109) | copy-start | bytes 1179652
  59.6 22.3 %all-to-all-start.2 = ((bf16[128,2,3,2,128]{4,3,1,2,0:T(2,128)(2,1)}), bf16[128,2,3,2,128]{4,3,1,2,0:T(2,128)(2,1)S(1)}, u32[]{:S(2)}, u32[]{:S(2)}) async-start(bf16[128,2,3,2,128]{4,3,1,2,0:T(2,128)(2,1)} %copy.166), calls=%async_computation.2 | async-start | bytes 786432 | tf_op jit(solution)/shard_map/all_to_all | solution.py:56
  82.6 11.5 %copy-start.73 = (bf16[2,1,128,128]{3,2,0,1:T(8,128)(2,1)S(1)}, bf16[2,1,128,128]{3,2,0,1:T(8,128)(2,1)}, u32[]{:S(2)}) copy-start(bf16[2,1,128,128]{3,2,0,1:T(8,128)(2,1)} %get-tuple-element.16) | copy-start | bytes 196612
  82.6 12.2 %copy-start.71 = (bf16[2,1,128,128]{3,2,0,1:T(8,128)(2,1)S(1)}, bf16[2,1,128,128]{3,2,0,1:T(8,128)(2,1)}, u32[]{:S(2)}) copy-start(bf16[2,1,128,128]{3,2,0,1:T(8,128)(2,1)} %get-tuple-element.14) | copy-start | bytes 196612
  82.7 17.5 %collective-permute-start = (bf16[2,1,2,3,2,128,128]{5,6,4,2,3,1,0:T(8,128)(2,1)S(1)}, bf16[2,1,2,3,2,128,128]{5,6,4,2,3,1,0:T(8,128)(2,1)S(1)}, u32[]{:S(2)}, u32[]{:S(2)}) collective-permute-start(bf16[2,1,2,3,2,128,128]{5,6,4,2,3,1,0:T(8,128)(2,1)S(1)} %pad_maximum_fusion.1), channel_id=1, source_target_pairs={{0,1},{1,2},{2,3},{4,5},{5,6},{6,7},{8,9},{9,10},{10,11},{12,13},{... | collective-permute-start | bytes 2359304 | tf_op jit(solution)/shard_map/ppermute | solution.py:45
  91.3 14.8 %collective-permute-start.1 = (bf16[2,1,2,3,2,128,128]{5,6,4,2,3,1,0:T(8,128)(2,1)S(1)}, bf16[2,1,2,3,2,128,128]{5,6,4,2,3,1,0:T(8,128)(2,1)S(1)}, u32[]{:S(2)}, u32[]{:S(2)}) collective-permute-start(bf16[2,1,2,3,2,128,128]{5,6,4,2,3,1,0:T(8,128)(2,1)S(1)} %pad_maximum_fusion.1), channel_id=1, source_target_pairs={{1,0},{2,1},{3,2},{5,4},{6,5},{7,6},{9,8},{10,9},{11,10},{13,12},{... | collective-permute-start | bytes 2359304 | tf_op jit(solution)/shard_map/ppermute | solution.py:46
  94.1 12.3 %copy-start.28 = (bf16[2,1,128,128]{3,2,0,1:T(8,128)(2,1)}, bf16[2,1,128,128]{3,2,0,1:T(8,128)(2,1)S(1)}, u32[]{:S(2)}) copy-start(bf16[2,1,128,128]{3,2,0,1:T(8,128)(2,1)S(1)} %get-tuple-element.12) | copy-start | bytes 196612
  111.1 2.8 %copy-start.3 = (bf16[1,2,2,128,128]{4,3,2,1,0:T(8,128)(2,1)S(1)}, bf16[1,2,2,128,128]{4,3,2,1,0:T(8,128)(2,1)}, u32[]{:S(2)}) copy-start(bf16[1,2,2,128,128]{4,3,2,1,0:T(8,128)(2,1)} %copy.206) | copy-start | bytes 393220
  111.1 2.8 %copy-start.8 = (bf16[1,2,2,128,128]{4,3,2,1,0:T(8,128)(2,1)S(1)}, bf16[1,2,2,128,128]{4,3,2,1,0:T(8,128)(2,1)}, u32[]{:S(2)}) copy-start(bf16[1,2,2,128,128]{4,3,2,1,0:T(8,128)(2,1)} %copy.198) | copy-start | bytes 393220
  111.1 2.8 %copy-start.10 = (bf16[1,2,2,128,128]{4,3,2,1,0:T(8,128)(2,1)S(1)}, bf16[1,2,2,128,128]{4,3,2,1,0:T(8,128)(2,1)}, u32[]{:S(2)}) copy-start(bf16[1,2,2,128,128]{4,3,2,1,0:T(8,128)(2,1)} %get-tuple-element.40) | copy-start | bytes 393220
  111.1 2.8 %copy-start.11 = (bf16[1,2,2,128,128]{4,3,2,1,0:T(8,128)(2,1)S(1)}, bf16[1,2,2,128,128]{4,3,2,1,0:T(8,128)(2,1)}, u32[]{:S(2)}) copy-start(bf16[1,2,2,128,128]{4,3,2,1,0:T(8,128)(2,1)} %get-tuple-element.41) | copy-start | bytes 393220
  115.6 3.7 %copy-start.7 = (bf16[1,2,2,128,128]{3,4,2,1,0:T(8,128)(2,1)S(1)}, bf16[1,2,2,128,128]{3,4,2,1,0:T(8,128)(2,1)}, u32[]{:S(2)}) copy-start(bf16[1,2,2,128,128]{3,4,2,1,0:T(8,128)(2,1)} %get-tuple-element.38) | copy-start | bytes 393220
  149.4 7.4 %copy-start.40 = (bf16[1,2,1,2,128,128]{4,5,3,1,2,0:T(8,128)(2,1)S(1)}, bf16[1,2,1,2,128,128]{4,5,3,1,2,0:T(8,128)(2,1)}, u32[]{:S(2)}) copy-start(bf16[1,2,1,2,128,128]{4,5,3,1,2,0:T(8,128)(2,1)} %get-tuple-element.43) | copy-start | bytes 393220
  149.4 7.5 %copy-start.39 = (bf16[1,2,1,2,128,128]{4,5,3,1,2,0:T(8,128)(2,1)S(1)}, bf16[1,2,1,2,128,128]{4,5,3,1,2,0:T(8,128)(2,1)}, u32[]{:S(2)}) copy-start(bf16[1,2,1,2,128,128]{4,5,3,1,2,0:T(8,128)(2,1)} %get-tuple-element.48) | copy-start | bytes 393220
  149.4 8.3 %copy-start.38 = (bf16[1,2,2,128,128]{3,4,2,1,0:T(8,128)(2,1)S(1)}, bf16[1,2,2,128,128]{3,4,2,1,0:T(8,128)(2,1)}, u32[]{:S(2)}) copy-start(bf16[1,2,2,128,128]{3,4,2,1,0:T(8,128)(2,1)} %get-tuple-element.47) | copy-start | bytes 393220
  149.7 8.8 %copy-start.37 = (bf16[1,2,2,128,128]{3,4,2,1,0:T(8,128)(2,1)S(1)}, bf16[1,2,2,128,128]{3,4,2,1,0:T(8,128)(2,1)}, u32[]{:S(2)}) copy-start(bf16[1,2,2,128,128]{3,4,2,1,0:T(8,128)(2,1)} %get-tuple-element.37) | copy-start | bytes 393220
  150.6 22.1 %all-to-all-start.3 = ((bf16[128,1,2,1,2,128]{5,4,2,3,1,0:T(2,128)(2,1)}), bf16[128,1,2,1,2,128]{5,4,2,3,1,0:T(2,128)(2,1)S(1)}, u32[]{:S(2)}, u32[]{:S(2)}) async-start(bf16[128,1,2,1,2,128]{5,4,2,3,1,0:T(2,128)(2,1)} %copy.185), calls=%async_computation.3 | async-start | bytes 262144 | tf_op jit(solution)/shard_map/all_to_all | solution.py:34
  160.0 6.5 %copy-start.21 = (bf16[1,2,128,384]{3,2,1,0:T(8,128)(2,1)S(1)}, bf16[1,2,128,384]{3,2,1,0:T(8,128)(2,1)}, u32[]{:S(2)}) copy-start(bf16[1,2,128,384]{3,2,1,0:T(8,128)(2,1)} %fusion.201) | copy-start | bytes 589828
  160.0 6.5 %copy-start.23 = (bf16[1,2,128,384]{3,2,1,0:T(8,128)(2,1)S(1)}, bf16[1,2,128,384]{3,2,1,0:T(8,128)(2,1)}, u32[]{:S(2)}) copy-start(bf16[1,2,128,384]{3,2,1,0:T(8,128)(2,1)} %get-tuple-element.118) | copy-start | bytes 589828
  160.0 6.5 %copy-start.24 = (bf16[1,2,128,384]{3,2,1,0:T(8,128)(2,1)S(1)}, bf16[1,2,128,384]{3,2,1,0:T(8,128)(2,1)}, u32[]{:S(2)}) copy-start(bf16[1,2,128,384]{3,2,1,0:T(8,128)(2,1)} %get-tuple-element.119) | copy-start | bytes 589828
  162.9 4.6 %copy-start.12 = (bf16[1,2,128,512]{3,2,1,0:T(8,128)(2,1)S(1)}, bf16[1,2,128,512]{3,2,1,0:T(8,128)(2,1)}, u32[]{:S(2)}) copy-start(bf16[1,2,128,512]{3,2,1,0:T(8,128)(2,1)} %fusion.203) | copy-start | bytes 786436
  162.9 4.6 %copy-start.14 = (bf16[1,2,128,512]{3,2,1,0:T(8,128)(2,1)S(1)}, bf16[1,2,128,512]{3,2,1,0:T(8,128)(2,1)}, u32[]{:S(2)}) copy-start(bf16[1,2,128,512]{3,2,1,0:T(8,128)(2,1)} %get-tuple-element.106) | copy-start | bytes 786436
  162.9 4.6 %copy-start.15 = (bf16[1,2,128,512]{3,2,1,0:T(8,128)(2,1)S(1)}, bf16[1,2,128,512]{3,2,1,0:T(8,128)(2,1)}, u32[]{:S(2)}) copy-start(bf16[1,2,128,512]{3,2,1,0:T(8,128)(2,1)} %get-tuple-element.107) | copy-start | bytes 786436
  167.5 2.3 copy-start.22
  167.6 2.3 copy-start.25
  169.9 17.3 %copy-start.4 = (bf16[1,2,2,128,128]{4,3,2,1,0:T(8,128)(2,1)S(1)}, bf16[1,2,2,128,128]{4,3,2,1,0:T(8,128)(2,1)}, u32[]{:S(2)}) copy-start(bf16[1,2,2,128,128]{4,3,2,1,0:T(8,128)(2,1)} %copy.206) | copy-start | bytes 393220
  172.6 27.7 %all-to-all-start.4 = ((bf16[128,1,2,2,2,128]{5,4,2,3,1,0:T(2,128)(2,1)}), bf16[128,1,2,2,2,128]{5,4,2,3,1,0:T(2,128)(2,1)S(1)}, u32[]{:S(2)}, u32[]{:S(2)}) async-start(bf16[128,1,2,2,2,128]{5,4,2,3,1,0:T(2,128)(2,1)} %copy.186), calls=%async_computation.4 | async-start | bytes 524288 | tf_op jit(solution)/shard_map/all_to_all | solution.py:34
  204.8 7.4 %copy-start.34 = (bf16[1,2,128,256]{2,3,1,0:T(8,128)(2,1)S(1)}, bf16[1,2,128,256]{2,3,1,0:T(8,128)(2,1)}, u32[]{:S(2)}) copy-start(bf16[1,2,128,256]{2,3,1,0:T(8,128)(2,1)} %fusion.157) | copy-start | bytes 393220
  204.8 7.4 %copy-start.41 = (bf16[1,2,128,256]{2,3,1,0:T(8,128)(2,1)S(1)}, bf16[1,2,128,256]{2,3,1,0:T(8,128)(2,1)}, u32[]{:S(2)}) copy-start(bf16[1,2,128,256]{2,3,1,0:T(8,128)(2,1)} %get-tuple-element.5) | copy-start | bytes 393220
  204.8 7.4 %copy-start.42 = (bf16[1,2,128,256]{2,3,1,0:T(8,128)(2,1)S(1)}, bf16[1,2,128,256]{2,3,1,0:T(8,128)(2,1)}, u32[]{:S(2)}) copy-start(bf16[1,2,128,256]{2,3,1,0:T(8,128)(2,1)} %get-tuple-element.6) | copy-start | bytes 393220
  204.9 9.9 %copy-start.35 = (bf16[1,2,1,2,128,128]{4,5,3,1,2,0:T(8,128)(2,1)S(1)}, bf16[1,2,1,2,128,128]{4,5,3,1,2,0:T(8,128)(2,1)}, u32[]{:S(2)}) copy-start(bf16[1,2,1,2,128,128]{4,5,3,1,2,0:T(8,128)(2,1)} %get-tuple-element.44) | copy-start | bytes 393220
  206.0 20.8 %all-to-all-start.5 = ((bf16[128,2,3,2,128]{4,1,3,2,0:T(2,128)(2,1)}), bf16[128,2,3,2,128]{4,1,3,2,0:T(2,128)(2,1)S(1)}, u32[]{:S(2)}, u32[]{:S(2)}) async-start(bf16[128,2,3,2,128]{4,1,3,2,0:T(2,128)(2,1)} %copy.191), calls=%async_computation.5 | async-start | bytes 786432 | tf_op jit(solution)/shard_map/all_to_all | solution.py:56
  212.2 5.3 %copy-start.19 = (bf16[1,2,2,640,128]{3,4,2,1,0:T(8,128)(2,1)S(1)}, bf16[1,2,2,640,128]{3,4,2,1,0:T(8,128)(2,1)}, u32[]{:S(2)}) copy-start(bf16[1,2,2,640,128]{3,4,2,1,0:T(8,128)(2,1)} %constant_dynamic-update-slice_fusion.62) | copy-start | bytes 1966084
  213.0 5.4 %copy-start.18 = (bf16[1,2,2,640,128]{4,3,2,1,0:T(8,128)(2,1)S(1)}, bf16[1,2,2,640,128]{4,3,2,1,0:T(8,128)(2,1)}, u32[]{:S(2)}) copy-start(bf16[1,2,2,640,128]{4,3,2,1,0:T(8,128)(2,1)} %constant_dynamic-update-slice_fusion.71) | copy-start | bytes 1966084
  217.5 16.8 %copy-start.70 = (bf16[1,2,128,128]{2,3,1,0:T(8,128)(2,1)S(1)}, bf16[1,2,128,128]{2,3,1,0:T(8,128)(2,1)}, u32[]{:S(2)}) copy-start(bf16[1,2,128,128]{2,3,1,0:T(8,128)(2,1)} %fusion.199) | copy-start | bytes 196612
  217.5 16.8 %copy-start.79 = (bf16[1,2,128,128]{2,3,1,0:T(8,128)(2,1)S(1)}, bf16[1,2,128,128]{2,3,1,0:T(8,128)(2,1)}, u32[]{:S(2)}) copy-start(bf16[1,2,128,128]{2,3,1,0:T(8,128)(2,1)} %get-tuple-element.161) | copy-start | bytes 196612
  217.5 16.8 %copy-start.80 = (bf16[1,2,128,128]{2,3,1,0:T(8,128)(2,1)S(1)}, bf16[1,2,128,128]{2,3,1,0:T(8,128)(2,1)}, u32[]{:S(2)}) copy-start(bf16[1,2,128,128]{2,3,1,0:T(8,128)(2,1)} %get-tuple-element.162) | copy-start | bytes 196612
  227.4 9.3 %collective-permute-start.2 = (bf16[1,1,2,3,2,128,128]{5,6,2,4,3,1,0:T(8,128)(2,1)S(1)}, bf16[1,1,2,3,2,128,128]{5,6,2,4,3,1,0:T(8,128)(2,1)S(1)}, u32[]{:S(2)}, u32[]{:S(2)}) collective-permute-start(bf16[1,1,2,3,2,128,128]{5,6,2,4,3,1,0:T(8,128)(2,1)S(1)} %bitcast.731), channel_id=1, source_target_pairs={{0,1},{1,2},{2,3},{4,5},{5,6},{6,7},{8,9},{9,10},{10,11},{12,13},{... | collective-permute-start | bytes 1179656 | tf_op jit(solution)/shard_map/ppermute | solution.py:45
  232.0 10.6 %collective-permute-start.3 = (bf16[1,1,2,3,2,128,128]{5,6,2,4,3,1,0:T(8,128)(2,1)S(1)}, bf16[1,1,2,3,2,128,128]{5,6,2,4,3,1,0:T(8,128)(2,1)S(1)}, u32[]{:S(2)}, u32[]{:S(2)}) collective-permute-start(bf16[1,1,2,3,2,128,128]{5,6,2,4,3,1,0:T(8,128)(2,1)S(1)} %bitcast.732), channel_id=1, source_target_pairs={{1,0},{2,1},{3,2},{5,4},{6,5},{7,6},{9,8},{10,9},{11,10},{13,12},{... | collective-permute-start | bytes 1179656 | tf_op jit(solution)/shard_map/ppermute | solution.py:46
  (63 other events, 78.6 us)
where the time goes:
time: 265 us; the launch traced here: 263 us
  local copies, waits for them, and re-layouts  82.1 us (31%)
  starting transfers between devices  77 us (29%)
  waiting for transfers between devices  69.9 us (26%)
  other arithmetic  18.8 us (7%)
  matrix products  14.1 us (5%)
    all_to_all x4, starting transfers between devices, exchange_in_pieces(): lax.all_to_all(section, axis, split_axis=0, concat_axis=0, tiled=True)  46.2 us
    unnamed x253, local copies, waits for them, and re-layouts  44.6 us
    all_to_all x4, waiting for transfers between devices, exchange_in_pieces(): lax.all_to_all(section, axis, split_axis=0, concat_axis=0, tiled=True)  31.4 us
    all_to_all x2, waiting for transfers between devices, to_energies(): lax.all_to_all(blocks, 'energy', split_axis=0, concat_axis=4, tiled=True)  21.6 us
    all_to_all x2, starting transfers between devices, to_energies(): lax.all_to_all(blocks, 'energy', split_axis=0, concat_axis=4, tiled=True)  13.4 us
    ppermute x2, starting transfers between devices, padded_2(): before = lax.ppermute(last, axis, up)  13.2 us
    ppermute x2, waiting for transfers between devices, padded_2(): after = lax.ppermute(initial, axis, down)  11.8 us
    squeeze x6, local copies, waits for them, and re-layouts, band_tile(): return (store[:, 2 + shift:2 + shift + row_count, offset], False)  7.55 us
  transfers between devices with their start and end apart: 10, of which 9 were waited for; matrix products, arithmetic and copies ran while one was open for 13% of the time, Pallas kernels for 0%

commit v1 on v0

v1 whole, which is shorter than its diff:
```python
import functools
import math

import jax
import jax.numpy as jnp
import numpy as np
from jax import lax
from jax.experimental import pallas as pl
from jax.experimental.pallas import tpu as pltpu
from jax.sharding import PartitionSpec as P

MESH = pl.DeviceIdType.MESH
F32 = jnp.float32
BF16 = jnp.bfloat16
VMEM = pl.BlockSpec(memory_space=pltpu.VMEM)


def exchange_kernel(count, halo, src, *rest):
    if halo == "none":
        dst, send_sem, recv_sem = rest
        landed = dst
    elif halo == "src":
        dst, rims, send_sem, recv_sem, rim_send, rim_recv = rest
        landed = dst
        before, after = rims.at[0], rims.at[1]
    else:
        dst, send_sem, recv_sem, rim_send, rim_recv = rest
        landed = dst.at[1]
        before, after = dst.at[0], dst.at[2]
    me = lax.axis_index("energy")
    section = lax.axis_index("space")
    sections = lax.axis_size("space")
    following = lax.rem(section + 1, sections)
    preceding = lax.rem(section + sections - 1, sections)

    barrier = pltpu.get_barrier_semaphore()

    def greet(k, carry):
        peer = lax.rem(me + k, count)
        pl.semaphore_signal(barrier, inc=1, device_id={"energy": peer}, device_id_type=MESH)
        return carry

    lax.fori_loop(1, count, greet, 0)
    greeted = count - 1
    if halo != "none":
        for other in (following, preceding):
            pl.semaphore_signal(barrier, inc=1, device_id={"space": other}, device_id_type=MESH)
        greeted += 2
    pl.semaphore_wait(barrier, greeted)

    def rim_copies(block):
        to_following = pltpu.make_async_remote_copy(
            block, before, rim_send.at[0], rim_recv.at[0],
            device_id={"space": following}, device_id_type=MESH)
        to_preceding = pltpu.make_async_remote_copy(
            block, after, rim_send.at[1], rim_recv.at[1],
            device_id={"space": preceding}, device_id_type=MESH)
        return (to_following, to_preceding)

    def send(k, carry):
        peer = lax.rem(me + k, count)
        pltpu.make_async_remote_copy(
            src.at[peer], landed.at[me], send_sem, recv_sem,
            device_id={"energy": peer}, device_id_type=MESH).start()
        return carry

    if halo == "src":
        rims_sent = rim_copies(src)
        for copy in rims_sent:
            copy.start()
    lax.fori_loop(1, count, send, 0)
    landed[pl.ds(me, 1)] = src[pl.ds(me, 1)]
    some = pl.ds(0, count - 1)
    everything = pltpu.make_async_remote_copy(
        src.at[some], landed.at[some], send_sem, recv_sem,
        device_id={"energy": lax.rem(me + 1, count)}, device_id_type=MESH)
    everything.wait_recv()
    if halo == "dst":
        rims_sent = rim_copies(landed)
        for copy in rims_sent:
            copy.start()
    everything.wait_send()
    if halo != "none":
        for copy in rims_sent:
            copy.wait()


def exchange(blocks, halo, name):
    count = blocks.shape[0]
    slab = jax.ShapeDtypeStruct(blocks.shape, blocks.dtype)
    sems = [pltpu.SemaphoreType.DMA, pltpu.SemaphoreType.DMA]
    rim_sems = [pltpu.SemaphoreType.DMA((2,)), pltpu.SemaphoreType.DMA((2,))]
    if halo == "none":
        out_shape, scratch = slab, sems
    elif halo == "src":
        out_shape = (slab, jax.ShapeDtypeStruct((2, *blocks.shape), blocks.dtype))
        scratch = sems + rim_sems
    else:
        out_shape = jax.ShapeDtypeStruct((3, *blocks.shape), blocks.dtype)
        scratch = sems + rim_sems
    return pl.pallas_call(
        functools.partial(exchange_kernel, count, halo),
        out_shape=out_shape,
        in_specs=[VMEM],
        out_specs=jax.tree.map(lambda _: VMEM, out_shape),
        scratch_shapes=scratch,
        compiler_params=pltpu.CompilerParams(collective_id=name, has_side_effects=True),
    )(blocks)


def dot(left, right, flipped=False):
    return lax.dot_general(
        left, right, (((1,), (1 if flipped else 0,)), ((), ())), preferred_element_type=F32)


def halves(values):
    upper = values.astype(BF16)
    return upper, (values - upper.astype(F32)).astype(BF16)


def wave_tables(points):
    angle = 2.0 * math.pi * np.outer(np.arange(points) + 0.5, np.arange(points)) / (2 * points)
    cos, sin = np.cos(angle), np.sin(angle)
    forward = np.concatenate([cos, sin], axis=0)
    return halves_of(forward), halves_of(cos.T), halves_of(sin.T)


def halves_of(table):
    upper = table.astype(jnp.bfloat16)
    lower = (table - upper.astype(np.float64)).astype(jnp.bfloat16)
    return np.stack([upper, lower])


def waves(forward, re, im):
    points = re.shape[0]
    both = jnp.concatenate([re, im], axis=1)
    spectrum = dot(forward[0], both) + dot(forward[1], both)
    width = re.shape[1]
    return (spectrum[:points, :width], spectrum[points:, width:],
            spectrum[:points, width:], spectrum[points:, :width])


def unwave(table, values):
    upper, lower = halves(values)
    return dot(table[0], upper) + dot(table[0], lower) + dot(table[1], upper)


def correlate_kernel(scale, greens, forward, back_cos, out):
    for tile in range(greens.shape[0] // 2):
        a, b, c, d = waves(forward, greens[2 * tile], greens[2 * tile + 1])
        product_re = (a - b) * (a + b) - (c - d) * (c + d)
        product_im = 2.0 * (a * c + b * d)
        both = unwave(back_cos, jnp.concatenate([product_re, product_im], axis=1)) * scale
        width = a.shape[1]
        out[2 * tile] = both[:, :width].astype(BF16)
        out[2 * tile + 1] = both[:, width:].astype(BF16)


def convolve_kernel(scale, row_count, starts, greens, screened, forward, back_cos, back_sin, out):
    per_row = greens.shape[0] // (2 * row_count)
    points = greens.shape[1]
    energies = lax.broadcasted_iota(jnp.int32, (points, 2 * greens.shape[2]), 0)
    for tile in range(greens.shape[0] // 2):
        a, b, c, d = waves(forward, greens[2 * tile], greens[2 * tile + 1])
        a2, b2, c2, d2 = waves(forward, screened[2 * tile], screened[2 * tile + 1])
        even_re = (a * a2 - c * c2) + (b * b2 - d * d2)
        even_im = (a * c2 + c * a2) - (b * d2 + d * b2)
        odd_re = (a * b2 + c * d2) + (b * a2 + d * c2)
        odd_im = (c * b2 - a * d2) + (b * c2 - d * a2)
        both = unwave(back_cos, jnp.concatenate([even_re, even_im], axis=1))
        both = both + unwave(back_sin, jnp.concatenate([-odd_im, odd_re], axis=1))
        first = starts[tile // per_row]
        active = (energies >= first) & (energies < first + points // 2)
        both = jnp.where(active, both * scale, 0.0)
        width = a.shape[1]
        out[2 * tile] = both[:, :width].astype(BF16)
        out[2 * tile + 1] = both[:, width:].astype(BF16)


def screen_kernel(row_count, polar, coulomb, out, mixed):
    width = polar.shape[-1]
    for row in range(row_count):
        for extent in range(-2, 5):
            total = None
            for middle in range(-2, 3):
                second = extent - middle
                if not -2 <= second <= 2:
                    continue
                left = coulomb[2 + row, middle + 2]
                if second >= 0:
                    tile = polar[2 + row + middle, second]
                    term = dot(left, jnp.concatenate([tile[0], tile[1]], axis=1))
                else:
                    tile = polar[2 + row + extent, -second]
                    term = dot(left, jnp.concatenate([tile[0], tile[1]], axis=0), True)
                total = term if total is None else total + term
            lanes = pl.ds((extent + 2) * width, width)
            mixed[pl.ds(0, width), lanes] = total[:, :width].astype(BF16)
            mixed[pl.ds(width, width), lanes] = total[:, width:].astype(BF16)
        for column in range(3):
            right = jnp.concatenate([coulomb[2 + row + column, k] for k in range(5)], axis=1)
            result = dot(mixed[:, column * width:(column + 5) * width], right, True)
            out[row, column, 0] = result[:width].astype(BF16)
            out[row, column, 1] = result[width:].astype(BF16)


def tile_right(tile, flipped):
    re, im = tile[0], tile[1]
    if flipped:
        return jnp.concatenate(
            [jnp.concatenate([re, -im], axis=1), jnp.concatenate([im, re], axis=1)], axis=0)
    return jnp.concatenate(
        [jnp.concatenate([re, im], axis=1), jnp.concatenate([-im, re], axis=1)], axis=0)


def band(store, row, offset):
    if offset >= 0:
        return store[row, offset], False
    return store[row + offset, -offset], True


def dyson_kernel(row_count, coupling, greens, sigma, out):
    width = greens.shape[-1]
    for row in range(row_count):
        lefts = []
        for middle in range(-2, 3):
            tile, flipped = band(greens, 2 + row, middle)
            parts = [tile[0].T, tile[1].T] if flipped else [tile[0], tile[1]]
            lefts.append(jnp.concatenate(parts, axis=1))
        products = []
        for extent in range(-2, 5):
            total = None
            for middle in range(-2, 3):
                second = extent - middle
                if not -2 <= second <= 2:
                    continue
                tile, flipped = band(sigma, 2 + row + middle, second)
                term = dot(lefts[middle + 2], tile_right(tile, flipped), flipped)
                total = term if total is None else total + term
            products.append(total.astype(BF16))
        for column in range(3):
            total = None
            for extent in range(column - 2, column + 3):
                tile, flipped = band(greens, 2 + row + extent, column - extent)
                term = dot(products[extent + 2], tile_right(tile, flipped), flipped)
                total = term if total is None else total + term
            base = greens[2 + row, column]
            out[row, column, 0] = (base[0].astype(F32) + coupling * total[:, :width]).astype(BF16)
            out[row, column, 1] = (base[1].astype(F32) + coupling * total[:, width:]).astype(BF16)


def local_call(kernel, out_shape, specs, scratch=()):
    return pl.pallas_call(
        kernel, out_shape=jax.ShapeDtypeStruct(out_shape, BF16), in_specs=specs,
        out_specs=VMEM, scratch_shapes=list(scratch))


def window_of(blocks, section, sections):
    outside = jnp.stack([section > 0, section >= 0, section < sections - 1])
    blocks = jnp.where(outside[:, None, None, None, None], blocks, jnp.zeros((), blocks.dtype))
    count = blocks.shape[1]
    width = blocks.shape[-1]
    slabs = jnp.transpose(blocks.reshape(3, count, 12, width), (0, 2, 1, 3))
    return slabs.reshape(6, 3, 2, count, width)


def on_device(greens, coulomb, band_mask, window_lo):
    row_count = greens.shape[1]
    width = greens.shape[-1]
    rows_all = band_mask.shape[0]
    section = lax.axis_index("space")
    sections = lax.axis_size("space")
    energies = lax.axis_size("energy")
    first_row = section * row_count
    tile_rows = first_row + lax.broadcasted_iota(jnp.int32, (row_count, 3), 0)
    tile_offsets = lax.broadcasted_iota(jnp.int32, (row_count, 3), 1)
    kept_tiles = (tile_rows + tile_offsets < rows_all)[:, :, None, None, None]
    greens = jnp.where(kept_tiles, greens[0], jnp.zeros((), greens.dtype))

    coulomb_rows = lax.broadcasted_iota(jnp.int32, (rows_all, 5), 0)
    coulomb_offsets = lax.broadcasted_iota(jnp.int32, (rows_all, 5), 1) - 2
    inside = (
        (coulomb_rows + coulomb_offsets >= 0)
        & (coulomb_rows + coulomb_offsets < rows_all)
        & (band_mask > 0)
    )
    masked = jnp.where(inside[:, :, None, None], coulomb, jnp.zeros((), coulomb.dtype))
    padded = jnp.pad(masked, ((2, 2), (0, 0), (0, 0), (0, 0)))
    coulomb_window = lax.dynamic_slice_in_dim(padded, first_row, row_count + 4, 0)
    starts = lax.dynamic_slice_in_dim(window_lo, first_row, row_count, 0)

    slabs = row_count * 3 * 2
    message = (width, slabs // 4, 4, width)
    forward, back_cos, back_sin = wave_tables(energies)
    scale = 1.0 / (energies * math.sqrt(energies))

    def packed(tiles):
        return jnp.transpose(tiles.reshape(slabs, tiles.shape[-2], width), (1, 0, 2)).reshape(message)

    def by_slab(blocks):
        return jnp.transpose(blocks.reshape(energies, slabs, width), (1, 0, 2))

    element_shape = (slabs, energies, width)
    own = packed(greens)
    arrived, rims = exchange(own, "src", 0)
    elements = by_slab(arrived)
    polar = local_call(
        functools.partial(correlate_kernel, scale), element_shape, [VMEM] * 3,
    )(elements, forward, back_cos)
    polar_window = window_of(exchange(packed(polar), "dst", 1), section, sections)
    screened = local_call(
        functools.partial(screen_kernel, row_count), (row_count, 3, 2, width, width), [VMEM] * 2,
        [pltpu.VMEM((2 * width, 7 * width), BF16)],
    )(polar_window, coulomb_window)
    screen_elements = by_slab(exchange(packed(screened), "none", 2))
    sigma = local_call(
        functools.partial(convolve_kernel, scale, row_count), element_shape,
        [pl.BlockSpec(memory_space=pltpu.SMEM)] + [VMEM] * 5,
    )(starts, elements, screen_elements, forward, back_cos, back_sin)
    sigma_window = window_of(exchange(packed(sigma), "dst", 3), section, sections)
    green_window = window_of(jnp.stack([rims[0], own, rims[1]]), section, sections)
    updated = local_call(
        functools.partial(dyson_kernel, row_count, 1.0 / (5 * width)),
        (row_count, 3, 2, width, width), [VMEM] * 2,
    )(green_window, sigma_window)
    return updated[None]


def solution(mesh):
    return jax.shard_map(
        on_device,
        mesh=mesh,
        in_specs=(P("energy", "space", None, None, None, None), P(), P(), P()),
        out_specs=P("energy", "space", None, None, None, None),
        check_vma=False,
    )
```

time: 265 us -> 163 us (0.62)
  Pallas kernels: 0 us -> 139 us
  starting transfers between devices: 77 us -> 0 us
  waiting for transfers between devices: 69.9 us -> 0 us
  local copies, waits for them, and re-layouts: 82.1 us -> 15.8 us
  matrix products: 14.1 us -> 0 us
  other arithmetic: 18.8 us -> 7.28 us
    pallas_call x0 -> x8, Pallas kernels: none -> 139 us  [the longest x4 122 us: exchange(): pl.pallas_call(functools.partial(exchange_kernel, count, halo), out_shape...]
    all_to_all x6 -> x0, starting transfers between devices: 59.5 us -> none  [the longest x4 46.2 us: exchange_in_pieces(): lax.all_to_all(section, axis, split_axis=0, concat_axis=0, tiled=True)]
    all_to_all x6 -> x0, waiting for transfers between devices: 53.1 us -> none  [the longest x4 31.4 us: exchange_in_pieces(): lax.all_to_all(section, axis, split_axis=0, concat_axis=0, tiled=True)]
    unnamed x253 -> x6, local copies, waits for them, and re-layouts: 44.6 us -> 0.01 us
    squeeze x28 -> x0, local copies, waits for them, and re-layouts: 18.8 us -> none  [the longest x6 7.55 us: band_tile(): return (store[:, 2 + shift:2 + shift + row_count, offset], False)]
    ppermute x4 -> x0, starting transfers between devices: 17.5 us -> none  [the longest x2 13.2 us: padded_2(): before = lax.ppermute(last, axis, up)]
    ppermute x4 -> x0, waiting for transfers between devices: 16.8 us -> none  [the longest x2 11.8 us: padded_2(): after = lax.ppermute(initial, axis, down)]
    dot_general x30 -> x0, matrix products: 14.1 us -> none  [the longest x10 5.01 us: complex_joined(): jnp.einsum('ercik,erkj->ercij', wide_left, tall_right, preferred_element_...]
  transfers between devices with their start and end apart: 10 -> 0, of which waited for: 9 -> 0; matrix products, arithmetic and copies ran while one was open for 13% -> 0% of each run, Pallas kernels for 0% -> 0%
where the time goes in v1:
time: 163 us; the launch traced here: 162 us
  Pallas kernels  139 us (85%)
  local copies, waits for them, and re-layouts  15.8 us (10%)
  other arithmetic  7.28 us (4%)
    pallas_call x4, Pallas kernels, exchange(): pl.pallas_call(functools.partial(exchange_kernel, count, halo), out_shape...  122 us
    reshape x4, local copies, waits for them, and re-layouts, packed(): jnp.transpose(tiles.reshape(slabs, tiles.shape[-2], width), (1, 0, 2))  7.23 us
    select_n x3, other arithmetic, window_of(): jnp.where(outside[:, None, None, None, None], blocks, jnp.zeros((), block...  4.86 us
    pallas_call x1, Pallas kernels, on_device(): local_call(functools.partial(convolve_kernel, scale, row_count), element_...  4.81 us
    pallas_call x1, Pallas kernels, on_device(): local_call(functools.partial(dyson_kernel, row_count, 1.0 / (5 * width)),...  4.51 us
    pallas_call x1, Pallas kernels, on_device(): local_call(functools.partial(correlate_kernel, scale), element_shape, [VM...  4.11 us
    pallas_call x1, Pallas kernels, on_device(): local_call(functools.partial(screen_kernel, row_count), (row_count, 3, 2,...  3.91 us
    pallas_call x2, local copies, waits for them, and re-layouts, exchange(): pl.pallas_call(functools.partial(exchange_kernel, count, halo), out_shape...  3.62 us

profile of v1, /device:TPU:1, one launch (start us, length us, event | category | flops | bytes accessed | tf_op | source)
XLA Modules:
  0.0 162.4 jit_solution(8262207875933310003)
XLA Ops:
  0.0 0.7 fusion.3
  0.7 1.5 broadcast_select_fusion
  2.2 0.0 copy-start.1
  2.2 1.2 pad_dynamic-slice_fusion.coulomb
  3.4 0.1 add_compare_fusion
  3.4 0.1 broadcast_in_dim.61
  3.5 0.1 broadcast_in_dim.62
  3.6 0.0 copy-done.1
  3.6 0.1 bitcast_select_fusion
  3.7 1.1 copy.18.src
  4.8 35.1 %shard_map.73 = (bf16[128,3,4,128]{3,2,1,0:T(4,128)(2,1)}, bf16[2,128,3,4,128]{4,3,2,1,0:T(4,128)(2,1)}) custom-call(bf16[128,3,4,128]{3,2,1,0:T(4,128)(2,1)} %copy.18.src), custom_call_target="tpu_custom_call" | custom-call | tf_op jit(solution)/shard_map/pallas_call | solution.py:101
  39.9 1.8 %copy.21 = bf16[128,3,4,128]{3,0,2,1:T(8,128)(2,1)} copy(bf16[128,3,4,128]{3,2,1,0:T(4,128)(2,1)} %get-tuple-element.8) | data formatting | bytes 786432 | tf_op jit(solution)/shard_map/pallas_call | solution.py:101
  41.7 4.1 %shard_map.74 = bf16[12,128,128]{2,1,0:T(8,128)(2,1)} custom-call(bf16[12,128,128]{2,1,0:T(8,128)(2,1)} %bitcast.48, bf16[2,256,128]{2,1,0:T(8,128)(2,1)} %constant.10.clone.forward, bf16[2,128,128]{2,1,0:T(8,128)(2,1)} %constant.30.clone.back_cos), custom_call_target="tpu_custom_call" | custom-call | tf_op jit(solution)/shard_map/pallas_call | solution.py:307
  45.8 2.1 %copy.22.src = bf16[128,3,4,128]{3,2,1,0:T(4,128)(2,1)} copy(bf16[128,3,4,128]{3,0,2,1:T(8,128)(2,1)} %bitcast.55) | data formatting | bytes 786432 | tf_op jit(solution)/shard_map/reshape | solution.py:298
  47.8 32.0 %shard_map.75 = bf16[3,128,3,4,128]{4,3,2,1,0:T(4,128)(2,1)} custom-call(bf16[128,3,4,128]{3,2,1,0:T(4,128)(2,1)} %copy.22.src), custom_call_target="tpu_custom_call" | custom-call | tf_op jit(solution)/shard_map/pallas_call | solution.py:101
  79.8 0.1 pad_add_fusion
  79.9 1.8 %broadcast_select_fusion.2 = bf16[3,128,3,4,128]{4,3,2,1,0:T(4,128)(2,1)S(1)} fusion(bf16[3,128,3,4,128]{4,3,2,1,0:T(4,128)(2,1)} %shard_map.75, pred[3]{0:T(512)(128)(4,1)S(1)} %pad_add_fusion), kind=kLoop, calls=%fused_computation.4 | loop fusion | flops 589824 | bytes 2359299 | tf_op jit(solution)/shard_map/jit(_where)/select_n | solution.py:260
  81.7 1.3 copy.23
  83.0 3.9 %shard_map.76 = bf16[2,3,2,128,128]{4,3,2,1,0:T(8,128)(2,1)} custom-call(bf16[6,3,2,128,128]{4,3,2,1,0:T(8,128)(2,1)} %bitcast.43, bf16[6,5,128,128]{3,2,1,0:T(8,128)(2,1)} %pad_dynamic-slice_fusion.coulomb), custom_call_target="tpu_custom_call" | custom-call | tf_op jit(solution)/shard_map/pallas_call | solution.py:311
  87.0 0.0 copy-start.2
  87.0 2.1 %copy.24.src = bf16[128,3,4,128]{3,2,1,0:T(4,128)(2,1)} copy(bf16[128,3,4,128]{3,0,2,1:T(8,128)(2,1)} %bitcast.52) | data formatting | bytes 786432 | tf_op jit(solution)/shard_map/reshape | solution.py:298
  89.0 22.0 %shard_map.77 = bf16[128,3,4,128]{3,2,1,0:T(4,128)(2,1)} custom-call(bf16[128,3,4,128]{3,2,1,0:T(4,128)(2,1)} %copy.24.src), custom_call_target="tpu_custom_call" | custom-call | tf_op jit(solution)/shard_map/pallas_call | solution.py:101
  111.0 1.8 %copy.25 = bf16[128,3,4,128]{3,0,2,1:T(8,128)(2,1)} copy(bf16[128,3,4,128]{3,2,1,0:T(4,128)(2,1)} %shard_map.77) | data formatting | bytes 786432 | tf_op jit(solution)/shard_map/pallas_call | solution.py:101
  112.8 0.0 copy-done.2
  112.8 0.6 dynamic_slice.6.starts
  113.5 4.8 %shard_map.78 = bf16[12,128,128]{2,1,0:T(8,128)(2,1)} custom-call(s32[2]{0:T(128)} %dynamic_slice.6.starts, bf16[12,128,128]{2,1,0:T(8,128)(2,1)} %bitcast.49, bf16[12,128,128]{2,1,0:T(8,128)(2,1)} %bitcast.53, bf16[2,256,128]{2,1,0:T(8,128)(2,1)} %constant.10.clone.forward, bf16[2,128,128]{2,1,0:T(8,128)(2,1)} %constant.30.clone.back_cos, ...), custom_call_target="tpu_custom_call" | custom-call | tf_op jit(solution)/shard_map/pallas_call | solution.py:316
  118.3 2.0 %copy.26.src = bf16[128,3,4,128]{3,2,1,0:T(4,128)(2,1)} copy(bf16[128,3,4,128]{3,0,2,1:T(8,128)(2,1)} %bitcast.54) | data formatting | bytes 786432 | tf_op jit(solution)/shard_map/reshape | solution.py:298
  120.3 32.8 %shard_map.79 = bf16[3,128,3,4,128]{4,3,2,1,0:T(4,128)(2,1)} custom-call(bf16[128,3,4,128]{3,2,1,0:T(4,128)(2,1)} %copy.26.src), custom_call_target="tpu_custom_call" | custom-call | tf_op jit(solution)/shard_map/pallas_call | solution.py:101
  153.1 1.8 %broadcast_select_fusion.1 = bf16[3,128,3,4,128]{4,3,2,1,0:T(4,128)(2,1)S(1)} fusion(bf16[3,128,3,4,128]{4,3,2,1,0:T(4,128)(2,1)} %shard_map.79, pred[3]{0:T(512)(128)(4,1)S(1)} %pad_add_fusion), kind=kLoop, calls=%fused_computation.3 | loop fusion | flops 589824 | bytes 2359299 | tf_op jit(solution)/shard_map/jit(_where)/select_n | solution.py:260
  154.9 0.0 copy-start
  154.9 1.3 copy.27
  156.3 0.0 copy-done
  156.3 0.3 fusion.4
  156.5 0.1 copy.19
  156.6 0.1 copy.20
  156.7 1.2 maximum_select_fusion
  157.9 4.5 %shard_map.80 = bf16[2,3,2,128,128]{4,3,2,1,0:T(8,128)(2,1)} custom-call(bf16[6,3,2,128,128]{4,3,2,1,0:T(8,128)(2,1)} %bitcast.44, bf16[6,3,2,128,128]{4,3,2,1,0:T(8,128)(2,1)} %bitcast.45), custom_call_target="tpu_custom_call" | custom-call | tf_op jit(solution)/shard_map/pallas_call | solution.py:322
  (2 shorter events, 0.0 us)
Async XLA Ops:
  2.2 1.4 copy-start.1
  87.0 25.9 %copy-start.2 = (s32[8]{0:T(128)S(1)}, s32[8]{0:T(128)}, u32[]{:S(2)}) copy-start(s32[8]{0:T(128)} %param.10) | copy-start | bytes 100
  154.9 1.3 copy-start

commit v2 on v1

v2 whole, which is shorter than its diff:
```python
import functools
import math

import jax
import jax.numpy as jnp
import numpy as np
from jax import lax
from jax.experimental import pallas as pl
from jax.experimental.pallas import tpu as pltpu
from jax.sharding import PartitionSpec as P

MESH = pl.DeviceIdType.MESH
F32 = jnp.float32
BF16 = jnp.bfloat16
VMEM = pl.BlockSpec(memory_space=pltpu.VMEM)


def dot(left, right, flipped=False):
    return lax.dot_general(
        left, right, (((1,), (1 if flipped else 0,)), ((), ())), preferred_element_type=F32)


def halves(values):
    upper = values.astype(BF16)
    return upper, (values - upper.astype(F32)).astype(BF16)


def wave_tables(points):
    angle = 2.0 * math.pi * np.outer(np.arange(points) + 0.5, np.arange(points)) / (2 * points)
    cos, sin = np.cos(angle), np.sin(angle)
    forward = np.concatenate([cos, sin], axis=0)
    return halves_of(forward), halves_of(cos.T), halves_of(sin.T)


def halves_of(table):
    upper = table.astype(jnp.bfloat16)
    lower = (table - upper.astype(np.float64)).astype(jnp.bfloat16)
    return np.stack([upper, lower])


def waves(forward, re, im):
    points = re.shape[0]
    both = jnp.concatenate([re, im], axis=1)
    spectrum = dot(forward[0], both) + dot(forward[1], both)
    width = re.shape[1]
    return (spectrum[:points, :width], spectrum[points:, width:],
            spectrum[:points, width:], spectrum[points:, :width])


def unwave(table, values):
    upper, lower = halves(values)
    return dot(table[0], upper) + dot(table[0], lower) + dot(table[1], upper)


def tile_right(tile, flipped):
    re, im = tile[0], tile[1]
    if flipped:
        return jnp.concatenate(
            [jnp.concatenate([re, -im], axis=1), jnp.concatenate([im, re], axis=1)], axis=0)
    return jnp.concatenate(
        [jnp.concatenate([re, im], axis=1), jnp.concatenate([-im, re], axis=1)], axis=0)


def steps(count, body):
    lax.fori_loop(0, count, lambda k, carry: (body(k), carry)[1], 0)


def pack(tiles, blocks):
    def group(g):
        blocks[:, g] = jnp.transpose(tiles[pl.ds(4 * g, 4)], (1, 0, 2))
    steps(blocks.shape[1], group)


def unpack(blocks, tiles):
    def group(g):
        tiles[pl.ds(4 * g, 4)] = jnp.transpose(blocks[:, g], (1, 0, 2))
    steps(blocks.shape[1], group)


def far_first(k):
    return 4 + jnp.where(k % 2 == 1, -((k + 1) // 2), k // 2)


def offsets(k):
    return 1 - k // 64, far_first(k // 8 % 8), far_first(k % 8)


def update_kernel(
    coupling, greens, coulomb, mask, window_lo, forward, back_cos, back_sin, out,
    own, arrived, green_rims, polar_sent, polar_blocks, screen_sent, screen_blocks,
    sigma_sent, sigma_blocks, slabs, spectra, green_tiles, window, potential, mixed,
    send_sem, recv_sem, rim_send, rim_recv,
):
    count = lax.axis_size("energy")
    sections = lax.axis_size("space")
    me = lax.axis_index("energy")
    section = lax.axis_index("space")
    row_count, width = greens.shape[0] // 6, greens.shape[-1]
    rows_all = coulomb.shape[0]
    points = count
    first_row = section * row_count
    scale = 1.0 / (count * math.sqrt(count))
    my_x, my_z, my_y = me // 64, me // 8 % 8, me % 8
    has_before, has_after = section > 0, section < sections - 1
    some = pl.ds(0, count - 1)

    def partner(k):
        dx, dz, dy = offsets(k)
        return (my_x + dx) % 2 * 64 + (my_z + dz) % 8 * 8 + (my_y + dy) % 8

    def send_all(phase, source, landed):
        def send(k):
            peer = partner(k)
            pltpu.make_async_remote_copy(
                source.at[peer], landed.at[me], send_sem.at[phase], recv_sem.at[phase],
                device_id={"energy": peer}, device_id_type=MESH).start()
        steps(count - 1, send)
        landed[pl.ds(me, 1)] = source[pl.ds(me, 1)]

    def everything(phase, source, landed):
        return pltpu.make_async_remote_copy(
            source.at[some], landed.at[some], send_sem.at[phase], recv_sem.at[phase],
            device_id={"energy": (me + 1) % count}, device_id_type=MESH)

    def rims(phase, block, before, after):
        to_following = pltpu.make_async_remote_copy(
            block, before, rim_send.at[phase, 0], rim_recv.at[phase, 0],
            device_id={"space": (section + 1) % sections}, device_id_type=MESH)
        to_preceding = pltpu.make_async_remote_copy(
            block, after, rim_send.at[phase, 1], rim_recv.at[phase, 1],
            device_id={"space": (section + sections - 1) % sections}, device_id_type=MESH)
        return to_following, to_preceding

    def start_rims(pair):
        @pl.when(has_after)
        def _():
            pair[0].start()

        @pl.when(has_before)
        def _():
            pair[1].start()

    def end_rims(pair, before, after, tiles, rows):
        @pl.when(has_before)
        def _():
            pair[0].wait_recv()
            unpack(before, tiles.at[pl.ds(0, rows)])

        @pl.when(section == 0)
        def _():
            tiles[pl.ds(0, rows)] = jnp.zeros((rows, width, width), BF16)

        @pl.when(has_after)
        def _():
            pair[1].wait_recv()
            unpack(after, tiles.at[pl.ds(2 * rows, rows)])

        @pl.when(section == sections - 1)
        def _():
            tiles[pl.ds(2 * rows, rows)] = jnp.zeros((rows, width, width), BF16)

    def sent_rims(pair):
        @pl.when(has_after)
        def _():
            pair[0].wait_send()

        @pl.when(has_before)
        def _():
            pair[1].wait_send()

    barrier = pltpu.get_barrier_semaphore()
    steps(count - 1, lambda k: pl.semaphore_signal(
        barrier, inc=1, device_id={"energy": partner(k)}, device_id_type=MESH))
    for step in (1, sections - 1):
        pl.semaphore_signal(
            barrier, inc=1, device_id={"space": (section + step) % sections}, device_id_type=MESH)

    rows = 6 * row_count

    def keep(k):
        row, offset = k // 6, k % 6 // 2
        kept = (jnp.zeros((width, width), jnp.int32) + (first_row + row + offset)) < rows_all
        green_tiles[rows + k] = jnp.where(kept, greens[k], jnp.zeros((), BF16))
    steps(rows, keep)
    pack(green_tiles.at[pl.ds(rows, rows)], own)
    pl.semaphore_wait(barrier, count + 1)

    send_all(0, own, arrived)
    green_pair = rims(0, own, green_rims.at[0], green_rims.at[1])
    start_rims(green_pair)

    def keep_potential(k):
        row = first_row - 2 + k
        inside_row = jnp.clip(row, 0, rows_all - 1)
        for offset in range(5):
            column = row + offset - 2
            there = (row >= 0) & (row < rows_all) & (column >= 0) & (column < rows_all)
            flag = jnp.where(there, mask[inside_row, offset], 0)
            kept = (jnp.zeros((width, width), jnp.int32) + flag) > 0
            potential[k, :, offset * width:(offset + 1) * width] = jnp.where(
                kept, coulomb[inside_row, offset], jnp.zeros((), BF16))
    steps(row_count + 4, keep_potential)

    everything(0, own, arrived).wait_recv()
    unpack(arrived, slabs)

    def correlate(tile):
        a, b, c, d = waves(forward, slabs[2 * tile], slabs[2 * tile + 1])
        for part, value in enumerate((a, b, c, d)):
            spectra[tile, part] = value
        product_re = (a - b) * (a + b) - (c - d) * (c + d)
        product_im = 2.0 * (a * c + b * d)
        both = unwave(back_cos, jnp.concatenate([product_re, product_im], axis=1)) * scale
        slabs[2 * tile] = both[:, :width].astype(BF16)
        slabs[2 * tile + 1] = both[:, width:].astype(BF16)
    steps(rows // 2, correlate)
    pack(slabs, polar_sent)

    send_all(1, polar_sent, polar_blocks.at[1])
    end_rims(green_pair, green_rims.at[0], green_rims.at[1], green_tiles, rows)
    everything(1, polar_sent, polar_blocks.at[1]).wait_recv()
    polar_pair = rims(1, polar_blocks.at[1], polar_blocks.at[0], polar_blocks.at[2])
    start_rims(polar_pair)
    unpack(polar_blocks.at[1], window.at[pl.ds(rows, rows)])
    end_rims(polar_pair, polar_blocks.at[0], polar_blocks.at[2], window, rows)

    def tile_of(store, row, offset):
        return store[6 * row + 2 * offset], store[6 * row + 2 * offset + 1]

    def screen(row):
        for extent in range(-2, 5):
            total = None
            for middle in range(-2, 3):
                second = extent - middle
                if not -2 <= second <= 2:
                    continue
                left = potential[2 + row, :, (middle + 2) * width:(middle + 3) * width]
                if second >= 0:
                    right = jnp.concatenate(tile_of(window, 2 + row + middle, second), axis=1)
                    term = dot(left, right)
                else:
                    right = jnp.concatenate(tile_of(window, 2 + row + extent, -second), axis=0)
                    term = dot(left, right, True)
                total = term if total is None else total + term
            lanes = pl.ds((extent + 2) * width, width)
            mixed[pl.ds(0, width), lanes] = total[:, :width].astype(BF16)
            mixed[pl.ds(width, width), lanes] = total[:, width:].astype(BF16)
        for column in range(3):
            left = mixed[:, column * width:(column + 5) * width]
            result = dot(left, potential[2 + row + column], True)
            slabs[6 * row + 2 * column] = result[:width].astype(BF16)
            slabs[6 * row + 2 * column + 1] = result[width:].astype(BF16)
    steps(row_count, screen)
    pack(slabs, screen_sent)

    send_all(2, screen_sent, screen_blocks)
    everything(2, screen_sent, screen_blocks).wait_recv()
    unpack(screen_blocks, slabs)
    energies = lax.broadcasted_iota(jnp.int32, (points, 2 * width), 0)

    def convolve(tile):
        a, b, c, d = [spectra[tile, part] for part in range(4)]
        a2, b2, c2, d2 = waves(forward, slabs[2 * tile], slabs[2 * tile + 1])
        even_re = (a * a2 - c * c2) + (b * b2 - d * d2)
        even_im = (a * c2 + c * a2) - (b * d2 + d * b2)
        odd_re = (a * b2 + c * d2) + (b * a2 + d * c2)
        odd_im = (c * b2 - a * d2) + (b * c2 - d * a2)
        both = unwave(back_cos, jnp.concatenate([even_re, even_im], axis=1))
        both = both + unwave(back_sin, jnp.concatenate([-odd_im, odd_re], axis=1))
        first = window_lo[first_row + tile // 3]
        active = (energies >= first) & (energies < first + points // 2)
        both = jnp.where(active, both * scale, 0.0)
        slabs[2 * tile] = both[:, :width].astype(BF16)
        slabs[2 * tile + 1] = both[:, width:].astype(BF16)
    steps(rows // 2, convolve)
    pack(slabs, sigma_sent)

    send_all(3, sigma_sent, sigma_blocks.at[1])
    everything(3, sigma_sent, sigma_blocks.at[1]).wait_recv()
    sigma_pair = rims(2, sigma_blocks.at[1], sigma_blocks.at[0], sigma_blocks.at[2])
    start_rims(sigma_pair)
    unpack(sigma_blocks.at[1], window.at[pl.ds(rows, rows)])
    end_rims(sigma_pair, sigma_blocks.at[0], sigma_blocks.at[2], window, rows)

    def banded(store, row, offset):
        if offset >= 0:
            return tile_of(store, row, offset), False
        return tile_of(store, row + offset, -offset), True

    def dyson(row):
        lefts = []
        for middle in range(-2, 3):
            tile, flipped = banded(green_tiles, 2 + row, middle)
            parts = [tile[0].T, tile[1].T] if flipped else [tile[0], tile[1]]
            lefts.append(jnp.concatenate(parts, axis=1))
        products = []
        for extent in range(-2, 5):
            total = None
            for middle in range(-2, 3):
                second = extent - middle
                if not -2 <= second <= 2:
                    continue
                tile, flipped = banded(window, 2 + row + middle, second)
                term = dot(lefts[middle + 2], tile_right(tile, flipped), flipped)
                total = term if total is None else total + term
            products.append(total.astype(BF16))
        for column in range(3):
            total = None
            for extent in range(column - 2, column + 3):
                tile, flipped = banded(green_tiles, 2 + row + extent, column - extent)
                term = dot(products[extent + 2], tile_right(tile, flipped), flipped)
                total = term if total is None else total + term
            base = tile_of(green_tiles, 2 + row, column)
            for part in range(2):
                change = coupling * total[:, part * width:(part + 1) * width]
                out[6 * row + 2 * column + part] = (base[part].astype(F32) + change).astype(BF16)
    steps(row_count, dyson)

    for phase, source, landed in (
        (0, own, arrived), (1, polar_sent, polar_blocks.at[1]),
        (2, screen_sent, screen_blocks), (3, sigma_sent, sigma_blocks.at[1])):
        everything(phase, source, landed).wait_send()
    for pair in (green_pair, polar_pair, sigma_pair):
        sent_rims(pair)


def on_device(greens, coulomb, band_mask, window_lo):
    row_count = greens.shape[1]
    width = greens.shape[-1]
    count = lax.axis_size("energy")
    rows = 6 * row_count
    forward, back_cos, back_sin = wave_tables(count)
    block = (count, rows // 4, 4, width)
    smem = pl.BlockSpec(memory_space=pltpu.SMEM)
    updated = pl.pallas_call(
        functools.partial(update_kernel, 1.0 / (5 * width)),
        out_shape=jax.ShapeDtypeStruct((rows, width, width), BF16),
        in_specs=[VMEM, VMEM, smem, smem, VMEM, VMEM, VMEM],
        out_specs=VMEM,
        scratch_shapes=[
            pltpu.VMEM(block, BF16), pltpu.VMEM(block, BF16), pltpu.VMEM((2, *block), BF16),
            pltpu.VMEM(block, BF16), pltpu.VMEM((3, *block), BF16),
            pltpu.VMEM(block, BF16), pltpu.VMEM(block, BF16),
            pltpu.VMEM(block, BF16), pltpu.VMEM((3, *block), BF16),
            pltpu.VMEM((rows, width, width), BF16),
            pltpu.VMEM((rows // 2, 4, count, width), F32),
            pltpu.VMEM((3 * rows, width, width), BF16),
            pltpu.VMEM((3 * rows, width, width), BF16),
            pltpu.VMEM((row_count + 4, width, 5 * width), BF16),
            pltpu.VMEM((2 * width, 7 * width), BF16),
            pltpu.SemaphoreType.DMA((4,)), pltpu.SemaphoreType.DMA((4,)),
            pltpu.SemaphoreType.DMA((3, 2)), pltpu.SemaphoreType.DMA((3, 2)),
        ],
        compiler_params=pltpu.CompilerParams(collective_id=0, has_side_effects=True),
    )(greens.reshape(rows, width, width), coulomb, band_mask, window_lo, forward, back_cos, back_sin)
    return updated.reshape(greens.shape)


def solution(mesh):
    return jax.shard_map(
        on_device,
        mesh=mesh,
        in_specs=(P("energy", "space", None, None, None, None), P(), P(), P()),
        out_specs=P("energy", "space", None, None, None, None),
        check_vma=False,
    )
```

time: 163 us -> 99 us (0.61)
  Pallas kernels: 139 us -> 97 us
  local copies, waits for them, and re-layouts: 15.8 us -> 1.77 us
  other arithmetic: 7.28 us -> 0 us
    pallas_call x8 -> x1, Pallas kernels: 139 us -> 97 us  [on_device(): pl.pallas_call(functools.partial(update_kernel, 1.0 / (5 * width)), out_s...]
    reshape x4 -> x0, local copies, waits for them, and re-layouts: 7.23 us -> none  [packed(): jnp.transpose(tiles.reshape(slabs, tiles.shape[-2], width), (1, 0, 2))]
    select_n x5 -> x0, other arithmetic: 6.43 us -> none  [the longest x3 4.86 us: window_of(): jnp.where(outside[:, None, None, None, None], blocks, jnp.zeros((), block...]
    pallas_call x2 -> x0, local copies, waits for them, and re-layouts: 3.62 us -> none  [exchange(): pl.pallas_call(functools.partial(exchange_kernel, count, halo), out_shape...]
    select_n x2 -> x0, local copies, waits for them, and re-layouts: 2.61 us -> none  [window_of(): jnp.where(outside[:, None, None, None, None], blocks, jnp.zeros((), block...]
    dynamic_slice x2 -> x0, local copies, waits for them, and re-layouts: 1.81 us -> none  [the longest x1 1.17 us: on_device(): lax.dynamic_slice_in_dim(padded, first_row, row_count + 4, 0)]
    unnamed x6 -> x1, local copies, waits for them, and re-layouts: 0.01 us -> 1.77 us
where the time goes in v2:
time: 99 us; the launch traced here: 98.8 us
  Pallas kernels  97 us (98%)
  local copies, waits for them, and re-layouts  1.77 us (2%)
    pallas_call x1, Pallas kernels, on_device(): pl.pallas_call(functools.partial(update_kernel, 1.0 / (5 * width)), out_s...  97 us

profile of v2, /device:TPU:1, one launch (start us, length us, event | category | flops | bytes accessed | tf_op | source)
XLA Modules:
  0.0 98.8 jit_solution(3466496923965391424)
XLA Ops:
  0.0 97.0 %shard_map.73 = bf16[12,128,128]{2,1,0:T(8,128)(2,1)} custom-call(bf16[12,128,128]{2,1,0:T(8,128)(2,1)} %bitcast.3, bf16[8,5,128,128]{3,2,1,0:T(8,128)(2,1)} %coulomb.1, s32[8,5]{1,0:T(8,128)} %mask.1, s32[8]{0:T(128)} %window_lo.1, bf16[2,256,128]{2,1,0:T(8,128)(2,1)} %constant.6.clone.forward, bf16[2,128,128]{2,1,0:T(8,128)(2,1)} %constant.7.clone.back_cos, ...), custom_call_target="tpu_custom_call" | custom-call | tf_op jit(solution)/shard_map/pallas_call | solution.py:335
  97.0 1.8 %copy.9 = bf16[1,2,3,2,128,128]{5,4,3,2,1,0:T(8,128)(2,1)} copy(bf16[1,2,3,2,128,128]{5,4,3,2,1,0:T(8,128)(2,1)} %bitcast.2) | data formatting | bytes 786432

commit v3 on v2

--- a/solution.py
+++ b/solution.py
@@ -77,18 +77,14 @@
     steps(blocks.shape[1], group)
 
 
-def far_first(k):
-    return 4 + jnp.where(k % 2 == 1, -((k + 1) // 2), k // 2)
-
-
-def offsets(k):
-    return 1 - k // 64, far_first(k // 8 % 8), far_first(k % 8)
+FAR_FIRST = (4, 3, 5, 2, 6, 1, 7, 0)
 
 
 def update_kernel(
-    coupling, greens, coulomb, mask, window_lo, forward, back_cos, back_sin, out,
+    coupling, greens_in, coulomb_in, mask, window_lo, forward_in, cos_in, sin_in, out,
     own, arrived, green_rims, polar_sent, polar_blocks, screen_sent, screen_blocks,
     sigma_sent, sigma_blocks, slabs, spectra, green_tiles, window, potential, mixed,
+    greens, coulomb, forward, back_cos, back_sin, in_sem,
     send_sem, recv_sem, rim_send, rim_recv,
 ):
     count = lax.axis_size("energy")
@@ -104,17 +100,21 @@
     has_before, has_after = section > 0, section < sections - 1
     some = pl.ds(0, count - 1)
 
-    def partner(k):
-        dx, dz, dy = offsets(k)
-        return (my_x + dx) % 2 * 64 + (my_z + dz) % 8 * 8 + (my_y + dy) % 8
+    along_y = [(my_y + offset) % 8 for offset in FAR_FIRST]
+    along_z = [(my_z + offset) % 8 * 8 for offset in FAR_FIRST]
+    others = [
+        across + deep + high
+        for across in ((my_x + 1) % 2 * 64, my_x * 64) for deep in along_z for high in along_y
+    ][:-1]
+
+    def with_partners(act):
+        for peer in others:
+            act(peer)
 
     def send_all(phase, source, landed):
-        def send(k):
-            peer = partner(k)
-            pltpu.make_async_remote_copy(
-                source.at[peer], landed.at[me], send_sem.at[phase], recv_sem.at[phase],
-                device_id={"energy": peer}, device_id_type=MESH).start()
-        steps(count - 1, send)
+        with_partners(lambda peer: pltpu.make_async_remote_copy(
+            source.at[peer], landed.at[me], send_sem.at[phase], recv_sem.at[phase],
+            device_id={"energy": peer}, device_id_type=MESH).start())
         landed[pl.ds(me, 1)] = source[pl.ds(me, 1)]
 
     def everything(phase, source, landed):
@@ -169,13 +169,22 @@
             pair[1].wait_send()
 
     barrier = pltpu.get_barrier_semaphore()
-    steps(count - 1, lambda k: pl.semaphore_signal(
-        barrier, inc=1, device_id={"energy": partner(k)}, device_id_type=MESH))
+    with_partners(lambda peer: pl.semaphore_signal(
+        barrier, inc=1, device_id={"energy": peer}, device_id_type=MESH))
     for step in (1, sections - 1):
         pl.semaphore_signal(
             barrier, inc=1, device_id={"space": (section + step) % sections}, device_id_type=MESH)
 
+    loads = [
+        pltpu.make_async_copy(source, target, in_sem.at[k])
+        for k, (source, target) in enumerate((
+            (greens_in, greens), (coulomb_in, coulomb), (forward_in, forward),
+            (cos_in, back_cos), (sin_in, back_sin)))]
+    for load in loads:
+        load.start()
+
     rows = 6 * row_count
+    loads[0].wait()
 
     def keep(k):
         row, offset = k // 6, k % 6 // 2
@@ -183,11 +192,7 @@
         green_tiles[rows + k] = jnp.where(kept, greens[k], jnp.zeros((), BF16))
     steps(rows, keep)
     pack(green_tiles.at[pl.ds(rows, rows)], own)
-    pl.semaphore_wait(barrier, count + 1)
-
-    send_all(0, own, arrived)
-    green_pair = rims(0, own, green_rims.at[0], green_rims.at[1])
-    start_rims(green_pair)
+    loads[1].wait()
 
     def keep_potential(k):
         row = first_row - 2 + k
@@ -200,6 +205,13 @@
             potential[k, :, offset * width:(offset + 1) * width] = jnp.where(
                 kept, coulomb[inside_row, offset], jnp.zeros((), BF16))
     steps(row_count + 4, keep_potential)
+    for load in loads[2:]:
+        load.wait()
+    pl.semaphore_wait(barrier, count + 1)
+
+    send_all(0, own, arrived)
+    green_pair = rims(0, own, green_rims.at[0], green_rims.at[1])
+    start_rims(green_pair)
 
     everything(0, own, arrived).wait_recv()
     unpack(arrived, slabs)
@@ -332,10 +344,11 @@
     forward, back_cos, back_sin = wave_tables(count)
     block = (count, rows // 4, 4, width)
     smem = pl.BlockSpec(memory_space=pltpu.SMEM)
+    away = pl.BlockSpec(memory_space=pl.ANY)
     updated = pl.pallas_call(
         functools.partial(update_kernel, 1.0 / (5 * width)),
         out_shape=jax.ShapeDtypeStruct((rows, width, width), BF16),
-        in_specs=[VMEM, VMEM, smem, smem, VMEM, VMEM, VMEM],
+        in_specs=[away, away, smem, smem, away, away, away],
         out_specs=VMEM,
         scratch_shapes=[
             pltpu.VMEM(block, BF16), pltpu.VMEM(block, BF16), pltpu.VMEM((2, *block), BF16),
@@ -348,6 +361,9 @@
             pltpu.VMEM((3 * rows, width, width), BF16),
             pltpu.VMEM((row_count + 4, width, 5 * width), BF16),
             pltpu.VMEM((2 * width, 7 * width), BF16),
+            pltpu.VMEM((rows, width, width), BF16), pltpu.VMEM(coulomb.shape, BF16),
+            pltpu.VMEM(forward.shape, BF16), pltpu.VMEM(back_cos.shape, BF16),
+            pltpu.VMEM(back_sin.shape, BF16), pltpu.SemaphoreType.DMA((5,)),
             pltpu.SemaphoreType.DMA((4,)), pltpu.SemaphoreType.DMA((4,)),
             pltpu.SemaphoreType.DMA((3, 2)), pltpu.SemaphoreType.DMA((3, 2)),
         ],

time: 99 us -> 90.8 us (0.917)
  Pallas kernels: 97 us -> 88.8 us
    pallas_call x1, Pallas kernels: 97 us -> 88.8 us  [on_device(): pl.pallas_call(functools.partial(update_kernel, 1.0 / (5 * width)), out_s...]
where the time goes in v3:
time: 90.8 us; the launch traced here: 90.6 us
  Pallas kernels  88.8 us (98%)
  local copies, waits for them, and re-layouts  1.77 us (2%)
    pallas_call x1, Pallas kernels, on_device(): pl.pallas_call(functools.partial(update_kernel, 1.0 / (5 * width)), out_s...  88.8 us

profile of v3, /device:TPU:1, one launch (start us, length us, event | category | flops | bytes accessed | tf_op | source)
XLA Modules:
  0.0 90.6 jit_solution(3895169519271976169)
XLA Ops:
  0.0 88.8 %shard_map.73 = bf16[12,128,128]{2,1,0:T(8,128)(2,1)} custom-call(bf16[12,128,128]{2,1,0:T(8,128)(2,1)} %bitcast.3, bf16[8,5,128,128]{3,2,1,0:T(8,128)(2,1)} %coulomb_in.1, s32[8,5]{1,0:T(8,128)} %mask.1, s32[8]{0:T(128)} %window_lo.1, bf16[2,256,128]{2,1,0:T(8,128)(2,1)} %constant.6.clone.forward_in, bf16[2,128,128]{2,1,0:T(8,128)(2,1)} %constant.7.clone.cos_in, ...), custom_call_target="tpu_custom_call" | custom-call | tf_op jit(solution)/shard_map/pallas_call | solution.py:348
  88.8 1.8 %copy.9 = bf16[1,2,3,2,128,128]{5,4,3,2,1,0:T(8,128)(2,1)} copy(bf16[1,2,3,2,128,128]{5,4,3,2,1,0:T(8,128)(2,1)} %bitcast.2) | data formatting | bytes 786432

commit v4 on v3

--- a/solution.py
+++ b/solution.py
@@ -83,7 +83,7 @@
 def update_kernel(
     coupling, greens_in, coulomb_in, mask, window_lo, forward_in, cos_in, sin_in, out,
     own, arrived, green_rims, polar_sent, polar_blocks, screen_sent, screen_blocks,
-    sigma_sent, sigma_blocks, slabs, spectra, green_tiles, window, potential, mixed,
+    sigma_sent, sigma_blocks, slabs, spectra, green_tiles, window, potential, mixed, sums,
     greens, coulomb, forward, back_cos, back_sin, in_sem,
     send_sem, recv_sem, rim_send, rim_recv,
 ):
@@ -113,21 +113,35 @@
 
     def send_all(phase, source, landed):
         with_partners(lambda peer: pltpu.make_async_remote_copy(
-            source.at[peer], landed.at[me], send_sem.at[phase], recv_sem.at[phase],
+            source.at[peer], landed.at[me], send_sem.at[phase], recv_sem.at[phase, my_x],
             device_id={"energy": peer}, device_id_type=MESH).start())
         landed[pl.ds(me, 1)] = source[pl.ds(me, 1)]
 
-    def everything(phase, source, landed):
+    def arrival(phase, source, landed, half):
+        part = pl.ds(0, count // 2 - half)
         return pltpu.make_async_remote_copy(
-            source.at[some], landed.at[some], send_sem.at[phase], recv_sem.at[phase],
-            device_id={"energy": (me + 1) % count}, device_id_type=MESH)
-
-    def rims(phase, block, before, after):
+            source.at[part], landed.at[part], send_sem.at[phase],
+            recv_sem.at[phase, my_x if half else 1 - my_x],
+            device_id={"energy": others[0]}, device_id_type=MESH)
+
+    def wait_all(phase, source, landed):
+        for half in range(2):
+            arrival(phase, source, landed, half).wait_recv()
+
+    def sent_all(phase, source, landed):
+        pltpu.make_async_remote_copy(
+            source.at[some], landed.at[some], send_sem.at[phase], recv_sem.at[phase, 0],
+            device_id={"energy": others[0]}, device_id_type=MESH).wait_send()
+
+    def rims(phase, block, before, after, half):
+        part = pl.ds((my_x if half else 1 - my_x) * (count // 2), count // 2)
         to_following = pltpu.make_async_remote_copy(
-            block, before, rim_send.at[phase, 0], rim_recv.at[phase, 0],
+            block.at[part], before.at[part], rim_send.at[phase, 0, half],
+            rim_recv.at[phase, 0, half],
             device_id={"space": (section + 1) % sections}, device_id_type=MESH)
         to_preceding = pltpu.make_async_remote_copy(
-            block, after, rim_send.at[phase, 1], rim_recv.at[phase, 1],
+            block.at[part], after.at[part], rim_send.at[phase, 1, half],
+            rim_recv.at[phase, 1, half],
             device_id={"space": (section + sections - 1) % sections}, device_id_type=MESH)
         return to_following, to_preceding
 
@@ -140,10 +154,11 @@
         def _():
             pair[1].start()
 
-    def end_rims(pair, before, after, tiles, rows):
+    def end_rims(pairs, before, after, tiles, rows):
         @pl.when(has_before)
         def _():
-            pair[0].wait_recv()
+            for pair in pairs:
+                pair[0].wait_recv()
             unpack(before, tiles.at[pl.ds(0, rows)])
 
         @pl.when(section == 0)
@@ -152,21 +167,30 @@
 
         @pl.when(has_after)
         def _():
-            pair[1].wait_recv()
+            for pair in pairs:
+                pair[1].wait_recv()
             unpack(after, tiles.at[pl.ds(2 * rows, rows)])
 
         @pl.when(section == sections - 1)
         def _():
             tiles[pl.ds(2 * rows, rows)] = jnp.zeros((rows, width, width), BF16)
 
-    def sent_rims(pair):
-        @pl.when(has_after)
-        def _():
-            pair[0].wait_send()
-
-        @pl.when(has_before)
-        def _():
-            pair[1].wait_send()
+    def sent_rims(pairs):
+        for pair in pairs:
+            @pl.when(has_after)
+            def _():
+                pair[0].wait_send()
+
+            @pl.when(has_before)
+            def _():
+                pair[1].wait_send()
+
+    def wait_and_pass_on(phase, rim_phase, source, blocks):
+        pairs = [rims(rim_phase, blocks.at[1], blocks.at[0], blocks.at[2], k) for k in range(2)]
+        for half in range(2):
+            arrival(phase, source, blocks.at[1], half).wait_recv()
+            start_rims(pairs[half])
+        return pairs
 
     barrier = pltpu.get_barrier_semaphore()
     with_partners(lambda peer: pl.semaphore_signal(
@@ -210,10 +234,11 @@
     pl.semaphore_wait(barrier, count + 1)
 
     send_all(0, own, arrived)
-    green_pair = rims(0, own, green_rims.at[0], green_rims.at[1])
-    start_rims(green_pair)
-
-    everything(0, own, arrived).wait_recv()
+    green_pairs = [rims(0, own, green_rims.at[0], green_rims.at[1], k) for k in range(2)]
+    for pair in green_pairs:
+        start_rims(pair)
+
+    wait_all(0, own, arrived)
     unpack(arrived, slabs)
 
     def correlate(tile):
@@ -229,31 +254,53 @@
     pack(slabs, polar_sent)
 
     send_all(1, polar_sent, polar_blocks.at[1])
-    end_rims(green_pair, green_rims.at[0], green_rims.at[1], green_tiles, rows)
-    everything(1, polar_sent, polar_blocks.at[1]).wait_recv()
-    polar_pair = rims(1, polar_blocks.at[1], polar_blocks.at[0], polar_blocks.at[2])
-    start_rims(polar_pair)
+    end_rims(green_pairs, green_rims.at[0], green_rims.at[1], green_tiles, rows)
+    polar_pairs = wait_and_pass_on(1, 1, polar_sent, polar_blocks)
     unpack(polar_blocks.at[1], window.at[pl.ds(rows, rows)])
-    end_rims(polar_pair, polar_blocks.at[0], polar_blocks.at[2], window, rows)
 
     def tile_of(store, row, offset):
         return store[6 * row + 2 * offset], store[6 * row + 2 * offset + 1]
 
-    def screen(row):
+    def partial_sum(row, extent, term, own_rows):
+        total = None
+        for middle in range(-2, 3):
+            stored = row + min(middle, extent)
+            if abs(extent - middle) <= 2 and (0 <= stored < row_count) == own_rows:
+                value = term(row, extent, middle)
+                total = value if total is None else total + value
+        return total
+
+    def sum_own(term):
+        for row in range(row_count):
+            for extent in range(-2, 5):
+                value = partial_sum(row, extent, term, True)
+                if value is not None:
+                    sums[row, extent + 2] = value
+
+    def sum_rest(row, extent, term):
+        value = partial_sum(row, extent, term, False)
+        has_own = any(
+            abs(extent - m) <= 2 and 0 <= row + min(m, extent) < row_count for m in range(-2, 3))
+        if not has_own:
+            return value
+        held = sums[row, extent + 2]
+        return held if value is None else held + value
+
+    def screen_term(row, extent, middle):
+        left = potential[2 + row, :, (middle + 2) * width:(middle + 3) * width]
+        second = extent - middle
+        if second >= 0:
+            tile = tile_of(window, 2 + row + middle, second)
+            return dot(left, jnp.concatenate(tile, axis=1))
+        tile = tile_of(window, 2 + row + extent, -second)
+        return dot(left, jnp.concatenate(tile, axis=0), True)
+
+    sum_own(screen_term)
+    end_rims(polar_pairs, polar_blocks.at[0], polar_blocks.at[2], window, rows)
+
+    for row in range(row_count):
         for extent in range(-2, 5):
-            total = None
-            for middle in range(-2, 3):
-                second = extent - middle
-                if not -2 <= second <= 2:
-                    continue
-                left = potential[2 + row, :, (middle + 2) * width:(middle + 3) * width]
-                if second >= 0:
-                    right = jnp.concatenate(tile_of(window, 2 + row + middle, second), axis=1)
-                    term = dot(left, right)
-                else:
-                    right = jnp.concatenate(tile_of(window, 2 + row + extent, -second), axis=0)
-                    term = dot(left, right, True)
-                total = term if total is None else total + term
+            total = sum_rest(row, extent, screen_term)
             lanes = pl.ds((extent + 2) * width, width)
             mixed[pl.ds(0, width), lanes] = total[:, :width].astype(BF16)
             mixed[pl.ds(width, width), lanes] = total[:, width:].astype(BF16)
@@ -262,11 +309,10 @@
             result = dot(left, potential[2 + row + column], True)
             slabs[6 * row + 2 * column] = result[:width].astype(BF16)
             slabs[6 * row + 2 * column + 1] = result[width:].astype(BF16)
-    steps(row_count, screen)
     pack(slabs, screen_sent)
 
     send_all(2, screen_sent, screen_blocks)
-    everything(2, screen_sent, screen_blocks).wait_recv()
+    wait_all(2, screen_sent, screen_blocks)
     unpack(screen_blocks, slabs)
     energies = lax.broadcasted_iota(jnp.int32, (points, 2 * width), 0)
 
@@ -288,34 +334,30 @@
     pack(slabs, sigma_sent)
 
     send_all(3, sigma_sent, sigma_blocks.at[1])
-    everything(3, sigma_sent, sigma_blocks.at[1]).wait_recv()
-    sigma_pair = rims(2, sigma_blocks.at[1], sigma_blocks.at[0], sigma_blocks.at[2])
-    start_rims(sigma_pair)
+    sigma_pairs = wait_and_pass_on(3, 2, sigma_sent, sigma_blocks)
     unpack(sigma_blocks.at[1], window.at[pl.ds(rows, rows)])
-    end_rims(sigma_pair, sigma_blocks.at[0], sigma_blocks.at[2], window, rows)
 
     def banded(store, row, offset):
         if offset >= 0:
             return tile_of(store, row, offset), False
         return tile_of(store, row + offset, -offset), True
 
-    def dyson(row):
-        lefts = []
+    lefts = []
+    for row in range(row_count):
         for middle in range(-2, 3):
             tile, flipped = banded(green_tiles, 2 + row, middle)
             parts = [tile[0].T, tile[1].T] if flipped else [tile[0], tile[1]]
             lefts.append(jnp.concatenate(parts, axis=1))
-        products = []
-        for extent in range(-2, 5):
-            total = None
-            for middle in range(-2, 3):
-                second = extent - middle
-                if not -2 <= second <= 2:
-                    continue
-                tile, flipped = banded(window, 2 + row + middle, second)
-                term = dot(lefts[middle + 2], tile_right(tile, flipped), flipped)
-                total = term if total is None else total + term
-            products.append(total.astype(BF16))
+
+    def dyson_term(row, extent, middle):
+        tile, flipped = banded(window, 2 + row + middle, extent - middle)
+        return dot(lefts[5 * row + middle + 2], tile_right(tile, flipped), flipped)
+
+    sum_own(dyson_term)
+    end_rims(sigma_pairs, sigma_blocks.at[0], sigma_blocks.at[2], window, rows)
+
+    for row in range(row_count):
+        products = [sum_rest(row, extent, dyson_term).astype(BF16) for extent in range(-2, 5)]
         for column in range(3):
             total = None
             for extent in range(column - 2, column + 3):
@@ -326,14 +368,13 @@
             for part in range(2):
                 change = coupling * total[:, part * width:(part + 1) * width]
                 out[6 * row + 2 * column + part] = (base[part].astype(F32) + change).astype(BF16)
-    steps(row_count, dyson)
 
     for phase, source, landed in (
         (0, own, arrived), (1, polar_sent, polar_blocks.at[1]),
         (2, screen_sent, screen_blocks), (3, sigma_sent, sigma_blocks.at[1])):
-        everything(phase, source, landed).wait_send()
-    for pair in (green_pair, polar_pair, sigma_pair):
-        sent_rims(pair)
+        sent_all(phase, source, landed)
+    for pairs in (green_pairs, polar_pairs, sigma_pairs):
+        sent_rims(pairs)
 
 
 def on_device(greens, coulomb, band_mask, window_lo):
@@ -361,11 +402,12 @@
             pltpu.VMEM((3 * rows, width, width), BF16),
             pltpu.VMEM((row_count + 4, width, 5 * width), BF16),
             pltpu.VMEM((2 * width, 7 * width), BF16),
+            pltpu.VMEM((row_count, 7, width, 2 * width), F32),
             pltpu.VMEM((rows, width, width), BF16), pltpu.VMEM(coulomb.shape, BF16),
             pltpu.VMEM(forward.shape, BF16), pltpu.VMEM(back_cos.shape, BF16),
             pltpu.VMEM(back_sin.shape, BF16), pltpu.SemaphoreType.DMA((5,)),
-            pltpu.SemaphoreType.DMA((4,)), pltpu.SemaphoreType.DMA((4,)),
-            pltpu.SemaphoreType.DMA((3, 2)), pltpu.SemaphoreType.DMA((3, 2)),
+            pltpu.SemaphoreType.DMA((4,)), pltpu.SemaphoreType.DMA((4, 2)),
+            pltpu.SemaphoreType.DMA((3, 2, 2)), pltpu.SemaphoreType.DMA((3, 2, 2)),
         ],
         compiler_params=pltpu.CompilerParams(collective_id=0, has_side_effects=True),
     )(greens.reshape(rows, width, width), coulomb, band_mask, window_lo, forward, back_cos, back_sin)

time: 90.8 us -> 88.5 us (0.975)
  Pallas kernels: 88.8 us -> 86.5 us
    pallas_call x1, Pallas kernels: 88.8 us -> 86.5 us  [on_device(): pl.pallas_call(functools.partial(update_kernel, 1.0 / (5 * width)), out_s...]
where the time goes in v4:
time: 88.5 us; the launch traced here: 88.3 us
  Pallas kernels  86.5 us (98%)
  local copies, waits for them, and re-layouts  1.77 us (2%)
    pallas_call x1, Pallas kernels, on_device(): pl.pallas_call(functools.partial(update_kernel, 1.0 / (5 * width)), out_s...  86.5 us

profile of v4, /device:TPU:1, one launch (start us, length us, event | category | flops | bytes accessed | tf_op | source)
XLA Modules:
  0.0 88.3 jit_solution(4493726347766773783)
XLA Ops:
  0.0 86.5 %shard_map.73 = bf16[12,128,128]{2,1,0:T(8,128)(2,1)} custom-call(bf16[12,128,128]{2,1,0:T(8,128)(2,1)} %bitcast.3, bf16[8,5,128,128]{3,2,1,0:T(8,128)(2,1)} %coulomb_in.1, s32[8,5]{1,0:T(8,128)} %mask.1, s32[8]{0:T(128)} %window_lo.1, bf16[2,256,128]{2,1,0:T(8,128)(2,1)} %constant.6.clone.forward_in, bf16[2,128,128]{2,1,0:T(8,128)(2,1)} %constant.7.clone.cos_in, ...), custom_call_target="tpu_custom_call" | custom-call | tf_op jit(solution)/shard_map/pallas_call | solution.py:389
  86.5 1.8 %copy.9 = bf16[1,2,3,2,128,128]{5,4,3,2,1,0:T(8,128)(2,1)} copy(bf16[1,2,3,2,128,128]{5,4,3,2,1,0:T(8,128)(2,1)} %bitcast.2) | data formatting | bytes 786432

commit v5 on v4

--- a/solution.py
+++ b/solution.py
@@ -241,16 +241,22 @@
     wait_all(0, own, arrived)
     unpack(arrived, slabs)
 
-    def correlate(tile):
-        a, b, c, d = waves(forward, slabs[2 * tile], slabs[2 * tile + 1])
-        for part, value in enumerate((a, b, c, d)):
-            spectra[tile, part] = value
-        product_re = (a - b) * (a + b) - (c - d) * (c + d)
-        product_im = 2.0 * (a * c + b * d)
-        both = unwave(back_cos, jnp.concatenate([product_re, product_im], axis=1)) * scale
-        slabs[2 * tile] = both[:, :width].astype(BF16)
-        slabs[2 * tile + 1] = both[:, width:].astype(BF16)
-    steps(rows // 2, correlate)
+    def correlate(pair):
+        tiles = (2 * pair, 2 * pair + 1)
+        series = [(slabs[2 * tile], slabs[2 * tile + 1]) for tile in tiles]
+        results = []
+        for re, im in series:
+            a, b, c, d = waves(forward, re, im)
+            product_re = (a - b) * (a + b) - (c - d) * (c + d)
+            product_im = 2.0 * (a * c + b * d)
+            both = unwave(back_cos, jnp.concatenate([product_re, product_im], axis=1)) * scale
+            results.append((both.astype(BF16), (a, b, c, d)))
+        for tile, (both, values) in zip(tiles, results):
+            for part, value in enumerate(values):
+                spectra[tile, part] = value
+            slabs[2 * tile] = both[:, :width]
+            slabs[2 * tile + 1] = both[:, width:]
+    steps(rows // 4, correlate)
     pack(slabs, polar_sent)
 
     send_all(1, polar_sent, polar_blocks.at[1])
@@ -316,27 +322,29 @@
     unpack(screen_blocks, slabs)
     energies = lax.broadcasted_iota(jnp.int32, (points, 2 * width), 0)
 
-    def convolve(tile):
-        a, b, c, d = [spectra[tile, part] for part in range(4)]
-        a2, b2, c2, d2 = waves(forward, slabs[2 * tile], slabs[2 * tile + 1])
-        even_re = (a * a2 - c * c2) + (b * b2 - d * d2)
-        even_im = (a * c2 + c * a2) - (b * d2 + d * b2)
-        odd_re = (a * b2 + c * d2) + (b * a2 + d * c2)
-        odd_im = (c * b2 - a * d2) + (b * c2 - d * a2)
-        both = unwave(back_cos, jnp.concatenate([even_re, even_im], axis=1))
-        both = both + unwave(back_sin, jnp.concatenate([-odd_im, odd_re], axis=1))
-        first = window_lo[first_row + tile // 3]
-        active = (energies >= first) & (energies < first + points // 2)
-        both = jnp.where(active, both * scale, 0.0)
-        slabs[2 * tile] = both[:, :width].astype(BF16)
-        slabs[2 * tile + 1] = both[:, width:].astype(BF16)
-    steps(rows // 2, convolve)
+    def convolve(pair):
+        tiles = (2 * pair, 2 * pair + 1)
+        series = [(slabs[2 * tile], slabs[2 * tile + 1]) for tile in tiles]
+        results = []
+        for tile, (re, im) in zip(tiles, series):
+            a, b, c, d = [spectra[tile, part] for part in range(4)]
+            a2, b2, c2, d2 = waves(forward, re, im)
+            even_re = (a * a2 - c * c2) + (b * b2 - d * d2)
+            even_im = (a * c2 + c * a2) - (b * d2 + d * b2)
+            odd_re = (a * b2 + c * d2) + (b * a2 + d * c2)
+            odd_im = (c * b2 - a * d2) + (b * c2 - d * a2)
+            both = unwave(back_cos, jnp.concatenate([even_re, even_im], axis=1))
+            both = both + unwave(back_sin, jnp.concatenate([-odd_im, odd_re], axis=1))
+            first = window_lo[first_row + tile // 3]
+            active = (energies >= first) & (energies < first + points // 2)
+            results.append(jnp.where(active, both * scale, 0.0).astype(BF16))
+        for tile, both in zip(tiles, results):
+            slabs[2 * tile] = both[:, :width]
+            slabs[2 * tile + 1] = both[:, width:]
+    steps(rows // 4, convolve)
     pack(slabs, sigma_sent)
 
     send_all(3, sigma_sent, sigma_blocks.at[1])
-    sigma_pairs = wait_and_pass_on(3, 2, sigma_sent, sigma_blocks)
-    unpack(sigma_blocks.at[1], window.at[pl.ds(rows, rows)])
-
     def banded(store, row, offset):
         if offset >= 0:
             return tile_of(store, row, offset), False
@@ -348,6 +356,9 @@
             tile, flipped = banded(green_tiles, 2 + row, middle)
             parts = [tile[0].T, tile[1].T] if flipped else [tile[0], tile[1]]
             lefts.append(jnp.concatenate(parts, axis=1))
+
+    sigma_pairs = wait_and_pass_on(3, 2, sigma_sent, sigma_blocks)
+    unpack(sigma_blocks.at[1], window.at[pl.ds(rows, rows)])
 
     def dyson_term(row, extent, middle):
         tile, flipped = banded(window, 2 + row + middle, extent - middle)

time: 88.5 us -> 87.5 us (0.989)
  Pallas kernels: 86.5 us -> 85.5 us
    pallas_call x1, Pallas kernels: 86.5 us -> 85.5 us  [on_device(): pl.pallas_call(functools.partial(update_kernel, 1.0 / (5 * width)), out_s...]
where the time goes in v5:
time: 87.5 us; the launch traced here: 87.3 us
  Pallas kernels  85.5 us (98%)
  local copies, waits for them, and re-layouts  1.77 us (2%)
    pallas_call x1, Pallas kernels, on_device(): pl.pallas_call(functools.partial(update_kernel, 1.0 / (5 * width)), out_s...  85.5 us
    unnamed x1, local copies, waits for them, and re-layouts  1.77 us

profile of v5, /device:TPU:1, one launch (start us, length us, event | category | flops | bytes accessed | tf_op | source)
XLA Modules:
  0.0 87.3 jit_solution(7340705306446517530)
XLA Ops:
  0.0 85.5 %shard_map.73 = bf16[12,128,128]{2,1,0:T(8,128)(2,1)} custom-call(bf16[12,128,128]{2,1,0:T(8,128)(2,1)} %bitcast.3, bf16[8,5,128,128]{3,2,1,0:T(8,128)(2,1)} %coulomb_in.1, s32[8,5]{1,0:T(8,128)} %mask.1, s32[8]{0:T(128)} %window_lo.1, bf16[2,256,128]{2,1,0:T(8,128)(2,1)} %constant.6.clone.forward_in, bf16[2,128,128]{2,1,0:T(8,128)(2,1)} %constant.7.clone.cos_in, ...), custom_call_target="tpu_custom_call" | custom-call | tf_op jit(solution)/shard_map/pallas_call | solution.py:400
  85.5 1.8 %copy.9 = bf16[1,2,3,2,128,128]{5,4,3,2,1,0:T(8,128)(2,1)} copy(bf16[1,2,3,2,128,128]{5,4,3,2,1,0:T(8,128)(2,1)} %bitcast.2) | data formatting | bytes 786432
